TPU v7x, 512 devices: a whole 4x4x16 slice. The times are simulated.
512 devices in a mesh: section: 16 (over z_lo, core), seq: 32 (over y, x, z_hi).
Axes of the slice: x: 4, y: 4, z: 16 (z_hi: 2, z_lo: 8; z = z_hi * 8 + z_lo), core: 2. Of those that a mesh axis runs over, the one named last changes fastest.
Arguments:
- query_row: bfloat16 [16, 8192, 512], P('section', 'seq'), may hold values from -80 to 80
- key_row: bfloat16 [16, 8192, 512], P('section', 'seq'), may hold values from -4 to 4
- value_row: bfloat16 [16, 8192, 512], P('section', 'seq'), may hold values from -6 to 6
- cotangent_row: bfloat16 [16, 8192, 512], P('section', 'seq'), may hold values from -6 to 6
- query_col: bfloat16 [16, 8192, 512], P('section', 'seq'), may hold values from -80 to 80
- key_col: bfloat16 [16, 8192, 512], P('section', 'seq'), may hold values from -4 to 4
- value_col: bfloat16 [16, 8192, 512], P('section', 'seq'), may hold values from -6 to 6
- cotangent_col: bfloat16 [16, 8192, 512], P('section', 'seq'), may hold values from -6 to 6
Outputs:
- upstream: bfloat16 [16, 8192, 3072], P('section', 'seq')
All inputs are finite; a program needn't handle non-finite values.
Results may differ from a plain program's by a relative error of at most 0.013.
Values may be sent and summed in bfloat16 or wider, within the bound.
No kernel may reach another device: no remote copies, remote signals or barrier semaphores. Data moves between devices by JAX's collectives and lax.ppermute only.
A program may use at most 64 MiB of HBM per device.

v0:
```python
import jax
import jax.numpy as jnp
from jax import lax
from jax.sharding import PartitionSpec as P

H_ROW = 4
H_COL = 4
HD = 128
COLS = 256


def from_behind(value, axis, steps):
    count = lax.axis_size(axis)
    leading, last = (max(0, -steps), min(count, count - steps))
    return lax.ppermute(value, axis, [(source, source + steps) for source in range(leading, last)])


def attend_back(queries, keys_in, values, grad_out):
    length = queries.shape[1]
    scaling = queries.shape[3] ** (-0.5)
    scores = (
        jnp.einsum("blhe,bmhe->bhlm", queries, keys_in, preferred_element_type=jnp.float32)
        * scaling
    )
    causal = jnp.arange(length)[:, None] >= jnp.arange(length)[None, :]
    scores = jnp.where(causal, scores, -1e30)
    largest = jnp.max(scores, axis=-1, keepdims=True)
    weights = jnp.exp(scores - largest)
    probability = weights / jnp.sum(weights, axis=-1, keepdims=True)
    prob_low = probability.astype(jnp.bfloat16)
    attended = jnp.einsum("bhlm,bmhe->blhe", prob_low, values, preferred_element_type=jnp.float32)
    inner_sum = jnp.sum(grad_out.astype(jnp.float32) * attended, axis=-1)
    grad_probs = jnp.einsum("blhe,bmhe->bhlm", grad_out, values, preferred_element_type=jnp.float32)
    grad_scores = (
        probability * (grad_probs - jnp.transpose(inner_sum, (0, 2, 1))[..., None]) * scaling
    )
    grad_low = grad_scores.astype(jnp.bfloat16)
    grad_query = jnp.einsum(
        "bhlm,bmhe->blhe", grad_low, keys_in, preferred_element_type=jnp.float32
    )
    grad_key = jnp.einsum("bhlm,blhe->bmhe", grad_low, queries, preferred_element_type=jnp.float32)
    grad_value = jnp.einsum(
        "bhlm,blhe->bmhe", prob_low, grad_out, preferred_element_type=jnp.float32
    )
    return (
        grad_query.astype(jnp.bfloat16),
        grad_key.astype(jnp.bfloat16),
        grad_value.astype(jnp.bfloat16),
    )


def row_grads(query_row, key_row, value_row, cotangent_row):
    tokens_dev, width = query_row.shape

    def as_rows(block):
        return block.reshape(tokens_dev // COLS, COLS, H_ROW, HD)

    result = attend_back(
        as_rows(query_row), as_rows(key_row), as_rows(value_row), as_rows(cotangent_row)
    )
    return jnp.stack([piece.reshape(tokens_dev, width) for piece in result], 1)


def col_work(pieces):
    query_col, key_col, value_col, cotangent_col = pieces
    grid_rows, single, columns, width = query_col.shape

    def as_cols(block):
        return jnp.transpose(block.reshape(grid_rows, columns, H_COL, HD), (1, 0, 2, 3))

    result = attend_back(
        as_cols(query_col), as_cols(key_col), as_cols(value_col), as_cols(cotangent_col)
    )
    return tuple(
        (
            jnp.transpose(piece, (1, 0, 2, 3)).reshape(grid_rows, single, columns, width)
            for piece in result
        )
    )


def col_grads(query_col, key_col, value_col, cotangent_col):
    tokens_dev, width = query_col.shape
    groups = lax.axis_size("seq")
    col_group = COLS // groups

    def regroup(block):
        return block.reshape(tokens_dev // COLS, groups, col_group, width)

    worked = col_work(
        (
            lax.all_to_all(regroup(query_col), "seq", split_axis=1, concat_axis=0, tiled=True),
            lax.all_to_all(regroup(key_col), "seq", split_axis=1, concat_axis=0, tiled=True),
            lax.all_to_all(regroup(value_col), "seq", split_axis=1, concat_axis=0, tiled=True),
            lax.all_to_all(regroup(cotangent_col), "seq", split_axis=1, concat_axis=0, tiled=True),
        )
    )
    returned = (
        lax.all_to_all(worked[0], "seq", split_axis=0, concat_axis=1, tiled=True),
        lax.all_to_all(worked[1], "seq", split_axis=0, concat_axis=1, tiled=True),
        lax.all_to_all(worked[2], "seq", split_axis=0, concat_axis=1, tiled=True),
    )
    return jnp.stack([piece.reshape(tokens_dev, width) for piece in returned], 1)


def on_device(
    query_row, key_row, value_row, cotangent_row, query_col, key_col, value_col, cotangent_col
):
    tokens_dev = query_row.shape[1]
    row_part = row_grads(query_row[0], key_row[0], value_row[0], cotangent_row[0])
    col_part = col_grads(query_col[0], key_col[0], value_col[0], cotangent_col[0])
    local_pack = jnp.concatenate([row_part, col_part], axis=-1).reshape(tokens_dev, -1)
    packed = from_behind(local_pack, "section", -1)
    return packed[None]


def solution(mesh):
    return jax.shard_map(
        on_device,
        mesh=mesh,
        in_specs=(
            P("section", "seq", None),
            P("section", "seq", None),
            P("section", "seq", None),
            P("section", "seq", None),
            P("section", "seq", None),
            P("section", "seq", None),
            P("section", "seq", None),
            P("section", "seq", None),
        ),
        out_specs=P("section", "seq", None),
        check_vma=False,
    )
```

profile of v0, /device:TPU:1, one launch (start us, length us, event | category | flops | bytes accessed | tf_op | source)
XLA Modules:
  0.0 211.6 jit_solution(13821977781159745271)
XLA Ops:
  0.0 38.9 %all_to_all.28 = bf16[1,32,8,512]{3,2,0,1:T(8,128)(2,1)S(1)} all-to-all(bf16[1,32,8,512]{3,2,0,1:T(8,128)(2,1)} %bitcast.142), channel_id=1, replica_groups=mesh['section'=16,'seq'=32] {'seq'}, dimensions={1} | all-to-all | bytes 524288 | tf_op jit(solution)/shard_map/all_to_all | solution.py:95
  38.9 20.8 %all_to_all.29 = bf16[1,32,8,512]{3,2,0,1:T(8,128)(2,1)S(1)} all-to-all(bf16[1,32,8,512]{3,2,0,1:T(8,128)(2,1)} %bitcast.143), channel_id=1, replica_groups=mesh['section'=16,'seq'=32] {'seq'}, dimensions={1} | all-to-all | bytes 524288 | tf_op jit(solution)/shard_map/all_to_all | solution.py:93
  59.8 20.9 %all_to_all.30 = bf16[1,32,8,512]{3,2,0,1:T(8,128)(2,1)S(1)} all-to-all(bf16[1,32,8,512]{3,2,0,1:T(8,128)(2,1)} %bitcast.144), channel_id=1, replica_groups=mesh['section'=16,'seq'=32] {'seq'}, dimensions={1} | all-to-all | bytes 524288 | tf_op jit(solution)/shard_map/all_to_all | solution.py:92
  80.7 3.9 %all-to-all-start.3 = ((bf16[1,32,8,512]{3,2,0,1:T(8,128)(2,1)}), bf16[1,32,8,512]{3,2,0,1:T(8,128)(2,1)S(1)}, u32[]{:S(2)}, u32[]{:S(2)}) async-start(bf16[1,32,8,512]{3,2,0,1:T(8,128)(2,1)} %bitcast.28), calls=%async_computation.3 | async-start | bytes 524288 | tf_op jit(solution)/shard_map/all_to_all | solution.py:94
  84.6 0.3 fusion.13
  84.9 1.3 fusion.46
  86.2 0.3 fusion.20
  86.5 0.9 copy.136
  87.4 14.3 %all-to-all-done.3 = bf16[1,32,8,512]{3,2,0,1:T(8,128)(2,1)S(1)} async-done(((bf16[1,32,8,512]{3,2,0,1:T(8,128)(2,1)}), bf16[1,32,8,512]{3,2,0,1:T(8,128)(2,1)S(1)}, u32[]{:S(2)}, u32[]{:S(2)}) %all-to-all-start.3) | async-done | bytes 262176 | tf_op jit(solution)/shard_map/all_to_all | solution.py:94
  101.7 4.9 %all-to-all-start.6 = ((bf16[32,1,8,512]{3,2,1,0:T(8,128)(2,1)}), bf16[32,1,8,512]{3,2,1,0:T(8,128)(2,1)S(1)}, u32[]{:S(2)}, u32[]{:S(2)}) async-start(bf16[32,1,8,512]{3,2,1,0:T(8,128)(2,1)} %bitcast.119), calls=%async_computation.6 | async-start | bytes 524288 | tf_op jit(solution)/shard_map/all_to_all | solution.py:101
  106.6 0.5 fusion.16
  107.1 0.3 fusion.15
  107.3 0.0 copy-start
  107.4 0.0 copy-start.1
  107.4 0.0 copy-start.2
  107.4 0.2 fusion.19
  107.6 0.9 copy.137
  108.5 15.1 %all-to-all-done.6 = bf16[32,1,8,512]{3,2,1,0:T(8,128)(2,1)S(1)} async-done(((bf16[32,1,8,512]{3,2,1,0:T(8,128)(2,1)}), bf16[32,1,8,512]{3,2,1,0:T(8,128)(2,1)S(1)}, u32[]{:S(2)}, u32[]{:S(2)}) %all-to-all-start.6) | async-done | bytes 262176 | tf_op jit(solution)/shard_map/all_to_all | solution.py:101
  123.6 5.5 %all-to-all-start.5 = ((bf16[32,1,8,512]{3,2,1,0:T(8,128)(2,1)}), bf16[32,1,8,512]{3,2,1,0:T(8,128)(2,1)S(1)}, u32[]{:S(2)}, u32[]{:S(2)}) async-start(bf16[32,1,8,512]{3,2,1,0:T(8,128)(2,1)} %bitcast.120), calls=%async_computation.5 | async-start | bytes 524288 | tf_op jit(solution)/shard_map/all_to_all | solution.py:100
  129.1 0.0 copy-done
  129.1 0.1 copy.98
  129.2 0.0 copy-done.1
  129.2 0.1 copy.97
  129.4 0.0 copy-done.2
  129.4 0.1 copy.96
  129.5 1.5 fusion.47
  131.1 0.3 fusion.18
  131.3 0.9 copy.138
  132.2 13.8 %all-to-all-done.5 = bf16[32,1,8,512]{3,2,1,0:T(8,128)(2,1)S(1)} async-done(((bf16[32,1,8,512]{3,2,1,0:T(8,128)(2,1)}), bf16[32,1,8,512]{3,2,1,0:T(8,128)(2,1)S(1)}, u32[]{:S(2)}, u32[]{:S(2)}) %all-to-all-start.5) | async-done | bytes 262176 | tf_op jit(solution)/shard_map/all_to_all | solution.py:100
  146.0 7.6 %all-to-all-start.4 = ((bf16[32,1,8,512]{3,2,1,0:T(8,128)(2,1)}), bf16[32,1,8,512]{3,2,1,0:T(8,128)(2,1)S(1)}, u32[]{:S(2)}, u32[]{:S(2)}) async-start(bf16[32,1,8,512]{3,2,1,0:T(8,128)(2,1)} %bitcast.121), calls=%async_computation.4 | async-start | bytes 524288 | tf_op jit(solution)/shard_map/all_to_all | solution.py:99
  153.6 0.0 copy-start.3
  153.7 0.8 convolution_convert_fusion.4
  154.5 0.1 copy.60
  154.6 0.1 copy.72
  154.8 0.0 copy-done.3
  154.8 0.1 copy.99
  154.9 0.8 fusion.17
  155.7 1.6 fusion.7
  157.3 0.3 convolution_convert_fusion.5
  157.6 0.1 copy.71
  157.7 0.2 convolution_convert_fusion
  158.0 0.1 copy.70
  158.1 12.5 %all-to-all-done.4 = bf16[32,1,8,512]{3,2,1,0:T(8,128)(2,1)S(1)} async-done(((bf16[32,1,8,512]{3,2,1,0:T(8,128)(2,1)}), bf16[32,1,8,512]{3,2,1,0:T(8,128)(2,1)S(1)}, u32[]{:S(2)}, u32[]{:S(2)}) %all-to-all-start.4) | async-done | bytes 262176 | tf_op jit(solution)/shard_map/all_to_all | solution.py:99
  170.7 0.2 maximum_maximum_fusion
  170.9 0.7 copy.86
  171.6 16.2 %collective-permute-start = (bf16[256,3072]{0,1:T(8,128)(2,1)S(1)}, bf16[256,3072]{0,1:T(8,128)(2,1)S(1)}, u32[]{:S(2)}, u32[]{:S(2)}) collective-permute-start(bf16[256,3072]{0,1:T(8,128)(2,1)S(1)} %bitcast.122), channel_id=1, source_target_pairs={{32,0},{64,32},{96,64},{128,96},{160,128},{192,160},{224,192},{256... | collective-permute-start | bytes 4718600 | tf_op jit(solution)/shard_map/ppermute | solution.py:15
  187.8 22.0 %collective-permute-done = bf16[256,3072]{0,1:T(8,128)(2,1)S(1)} collective-permute-done((bf16[256,3072]{0,1:T(8,128)(2,1)S(1)}, bf16[256,3072]{0,1:T(8,128)(2,1)S(1)}, u32[]{:S(2)}, u32[]{:S(2)}) %collective-permute-start) | collective-permute-done | bytes 1572896 | tf_op jit(solution)/shard_map/ppermute | solution.py:15
  209.8 1.7 copy.87
  (2 shorter events, 0.0 us)
Async XLA Ops:
  80.7 21.0 %all-to-all-start.3 = ((bf16[1,32,8,512]{3,2,0,1:T(8,128)(2,1)}), bf16[1,32,8,512]{3,2,0,1:T(8,128)(2,1)S(1)}, u32[]{:S(2)}, u32[]{:S(2)}) async-start(bf16[1,32,8,512]{3,2,0,1:T(8,128)(2,1)} %bitcast.28), calls=%async_computation.3 | async-start | bytes 524288 | tf_op jit(solution)/shard_map/all_to_all | solution.py:94
  101.7 21.9 %all-to-all-start.6 = ((bf16[32,1,8,512]{3,2,1,0:T(8,128)(2,1)}), bf16[32,1,8,512]{3,2,1,0:T(8,128)(2,1)S(1)}, u32[]{:S(2)}, u32[]{:S(2)}) async-start(bf16[32,1,8,512]{3,2,1,0:T(8,128)(2,1)} %bitcast.119), calls=%async_computation.6 | async-start | bytes 524288 | tf_op jit(solution)/shard_map/all_to_all | solution.py:101
  107.3 21.7 %copy-start = (bf16[1,256,512]{2,1,0:T(8,128)(2,1)S(1)}, bf16[1,256,512]{2,1,0:T(8,128)(2,1)}, u32[]{:S(2)}) copy-start(bf16[1,256,512]{2,1,0:T(8,128)(2,1)} %param.11) | copy-start | bytes 786436
  107.4 21.9 %copy-start.1 = (bf16[1,256,512]{2,1,0:T(8,128)(2,1)S(1)}, bf16[1,256,512]{2,1,0:T(8,128)(2,1)}, u32[]{:S(2)}) copy-start(bf16[1,256,512]{2,1,0:T(8,128)(2,1)} %param.8) | copy-start | bytes 786436
  107.4 22.0 %copy-start.2 = (bf16[1,256,512]{2,1,0:T(8,128)(2,1)S(1)}, bf16[1,256,512]{2,1,0:T(8,128)(2,1)}, u32[]{:S(2)}) copy-start(bf16[1,256,512]{2,1,0:T(8,128)(2,1)} %param.9) | copy-start | bytes 786436
  123.6 22.5 %all-to-all-start.5 = ((bf16[32,1,8,512]{3,2,1,0:T(8,128)(2,1)}), bf16[32,1,8,512]{3,2,1,0:T(8,128)(2,1)S(1)}, u32[]{:S(2)}, u32[]{:S(2)}) async-start(bf16[32,1,8,512]{3,2,1,0:T(8,128)(2,1)} %bitcast.120), calls=%async_computation.5 | async-start | bytes 524288 | tf_op jit(solution)/shard_map/all_to_all | solution.py:100
  146.0 24.6 %all-to-all-start.4 = ((bf16[32,1,8,512]{3,2,1,0:T(8,128)(2,1)}), bf16[32,1,8,512]{3,2,1,0:T(8,128)(2,1)S(1)}, u32[]{:S(2)}, u32[]{:S(2)}) async-start(bf16[32,1,8,512]{3,2,1,0:T(8,128)(2,1)} %bitcast.121), calls=%async_computation.4 | async-start | bytes 524288 | tf_op jit(solution)/shard_map/all_to_all | solution.py:99
  153.6 1.1 copy-start.3
  171.6 38.2 %collective-permute-start = (bf16[256,3072]{0,1:T(8,128)(2,1)S(1)}, bf16[256,3072]{0,1:T(8,128)(2,1)S(1)}, u32[]{:S(2)}, u32[]{:S(2)}) collective-permute-start(bf16[256,3072]{0,1:T(8,128)(2,1)S(1)} %bitcast.122), channel_id=1, source_target_pairs={{32,0},{64,32},{96,64},{128,96},{160,128},{192,160},{224,192},{256... | collective-permute-start | bytes 4718600 | tf_op jit(solution)/shard_map/ppermute | solution.py:15
where the time goes:
time: 212 us
  blocking collectives  80.7 us (38%)
  waiting for transfers between devices  77.8 us (37%)
  starting transfers between devices  38 us (18%)
  matrix products  7.02 us (3%)
  local copies, waits for them, and re-layouts  6.16 us (3%)
    all_to_all x1, blocking collectives, col_grads(): lax.all_to_all(regroup(cotangent_col), 'seq', split_axis=1, concat_axis=0...  38.9 us
    ppermute x1, waiting for transfers between devices, from_behind(): lax.ppermute(value, axis, [(source, source + steps) for source in range(l...  22 us
    all_to_all x1, blocking collectives, col_grads(): lax.all_to_all(regroup(query_col), 'seq', split_axis=1, concat_axis=0, ti...  20.9 us
    all_to_all x1, blocking collectives, col_grads(): lax.all_to_all(regroup(key_col), 'seq', split_axis=1, concat_axis=0, tile...  20.8 us
    ppermute x1, starting transfers between devices, from_behind(): lax.ppermute(value, axis, [(source, source + steps) for source in range(l...  16.2 us
    all_to_all x1, waiting for transfers between devices, col_grads(): lax.all_to_all(worked[2], 'seq', split_axis=0, concat_axis=1, tiled=True)  15.1 us
    all_to_all x1, waiting for transfers between devices, col_grads(): lax.all_to_all(regroup(value_col), 'seq', split_axis=1, concat_axis=0, ti...  14.3 us
    all_to_all x1, waiting for transfers between devices, col_grads(): lax.all_to_all(worked[1], 'seq', split_axis=0, concat_axis=1, tiled=True)  13.8 us
  transfers between devices with their start and end apart: 5, of which 5 were waited for; matrix products, arithmetic and copies ran while one was open for 6% of the time, Pallas kernels for 0%

commit v1 on v0

v1 whole, which is shorter than its diff:
```python
import functools

import jax
import jax.numpy as jnp
from jax import lax
from jax.experimental import pallas as pl
from jax.experimental.pallas import tpu as pltpu
from jax.sharding import PartitionSpec as P

H_ROW = 4
H_COL = 4
HD = 128
COLS = 256


def from_behind(value, axis, steps):
    count = lax.axis_size(axis)
    leading, last = (max(0, -steps), min(count, count - steps))
    return lax.ppermute(value, axis, [(source, source + steps) for source in range(leading, last)])


def dot_nt(a, b):
    return lax.dot_general(a, b, (((1,), (1,)), ((), ())), preferred_element_type=jnp.float32)


def dot_tn(a, b):
    return lax.dot_general(a, b, (((0,), (0,)), ((), ())), preferred_element_type=jnp.float32)


def dot_nn(a, b):
    return lax.dot_general(a, b, (((1,), (0,)), ((), ())), preferred_element_type=jnp.float32)


def head_back(queries, keys, values, grad_out, allowed):
    scaling = HD ** (-0.5)
    scores = jnp.where(allowed, dot_nt(queries, keys) * scaling, -1e30)
    largest = jnp.max(scores, axis=-1, keepdims=True)
    weights = jnp.exp(scores - largest)
    probability = weights / jnp.sum(weights, axis=-1, keepdims=True)
    prob_low = probability.astype(jnp.bfloat16)
    grad_probs = dot_nt(grad_out, values)
    inner_sum = jnp.sum(prob_low.astype(jnp.float32) * grad_probs, axis=-1, keepdims=True)
    grad_low = (probability * (grad_probs - inner_sum) * scaling).astype(jnp.bfloat16)
    return (
        dot_nn(grad_low, keys).astype(jnp.bfloat16),
        dot_tn(grad_low, queries).astype(jnp.bfloat16),
        dot_tn(prob_low, grad_out).astype(jnp.bfloat16),
    )


def attend_kernel(group, q_ref, k_ref, v_ref, g_ref, dq_ref, dk_ref, dv_ref):
    tokens = q_ref.shape[0]
    query_at = lax.broadcasted_iota(jnp.int32, (tokens, tokens), 0)
    key_at = lax.broadcasted_iota(jnp.int32, (tokens, tokens), 1)
    allowed = query_at >= key_at
    if group > 1:
        allowed = allowed & ((query_at - key_at) % group == 0)
    dq, dk, dv = head_back(q_ref[...], k_ref[...], v_ref[...], g_ref[...], allowed)
    dq_ref[...] = dq
    dk_ref[...] = dk
    dv_ref[...] = dv


def attend_back(group, heads, operands, offsets):
    tokens = operands[0].shape[0]
    width = heads * HD

    def spec(offset):
        return pl.BlockSpec((tokens, HD), lambda h: (0, h + offset))

    pairs = heads * tokens * tokens
    return pl.pallas_call(
        functools.partial(attend_kernel, group),
        grid=(heads,),
        in_specs=[spec(offset) for offset in offsets],
        out_specs=[spec(0)] * 3,
        out_shape=[jax.ShapeDtypeStruct((tokens, width), jnp.bfloat16)] * 3,
        cost_estimate=pl.CostEstimate(
            flops=10 * pairs * HD, bytes_accessed=14 * tokens * width, transcendentals=pairs
        ),
    )(*operands)


def on_device(
    query_row, key_row, value_row, cotangent_row, query_col, key_col, value_col, cotangent_col
):
    tokens_dev, width = query_row.shape[1:]
    groups = lax.axis_size("seq")
    col_group = COLS // groups
    sent = jnp.concatenate([query_col[0], key_col[0], value_col[0], cotangent_col[0]], axis=-1)
    sent = sent.reshape(groups, col_group, 4 * width)
    arrived = lax.all_to_all(sent, "seq", split_axis=0, concat_axis=0, tiled=True)
    arrived = arrived.reshape(groups * col_group, 4 * width)

    row_part = attend_back(
        1, H_ROW, (query_row[0], key_row[0], value_row[0], cotangent_row[0]), (0, 0, 0, 0)
    )
    row_pack = from_behind(jnp.concatenate(row_part, axis=-1), "section", -1)

    col_part = attend_back(
        col_group, H_COL, (arrived,) * 4, (0, H_COL, 2 * H_COL, 3 * H_COL)
    )
    col_sent = jnp.concatenate(col_part, axis=-1).reshape(groups, col_group, 3 * width)
    col_pack = lax.all_to_all(col_sent, "seq", split_axis=0, concat_axis=0, tiled=True)
    col_pack = from_behind(col_pack.reshape(tokens_dev, 3 * width), "section", -1)
    pieces = []
    for i in range(3):
        pieces += [row_pack[:, i * width : (i + 1) * width], col_pack[:, i * width : (i + 1) * width]]
    return jnp.concatenate(pieces, axis=-1)[None]


def solution(mesh):
    return jax.shard_map(
        on_device,
        mesh=mesh,
        in_specs=(P("section", "seq", None),) * 8,
        out_specs=P("section", "seq", None),
        check_vma=False,
    )
```

time: 212 us -> 134 us (0.63)
  blocking collectives: 80.7 us -> 51.9 us
  starting transfers between devices: 38 us -> 12.7 us
  waiting for transfers between devices: 77.8 us -> 53 us
  Pallas kernels: 0 us -> 9.74 us
  matrix products: 7.02 us -> 0 us
  local copies, waits for them, and re-layouts: 6.16 us -> 1.29 us
  other arithmetic: 1.54 us -> 4.48 us
    all_to_all x4 -> x1, waiting for transfers between devices: 55.8 us -> 11.8 us  [on_device(): lax.all_to_all(col_sent, 'seq', split_axis=0, concat_axis=0, tiled=True)]
    all_to_all x3 -> x1, blocking collectives: 80.7 us -> 51.9 us  [on_device(): lax.all_to_all(sent, 'seq', split_axis=0, concat_axis=0, tiled=True)]
    ppermute x1 -> x2, waiting for transfers between devices: 22 us -> 41.3 us  [from_behind(): lax.ppermute(value, axis, [(source, source + steps) for source in range(l...]
    all_to_all x4 -> x1, starting transfers between devices: 21.9 us -> 3.91 us  [on_device(): lax.all_to_all(col_sent, 'seq', split_axis=0, concat_axis=0, tiled=True)]
    pallas_call x0 -> x2, Pallas kernels: none -> 9.74 us  [attend_back(): pl.pallas_call(functools.partial(attend_kernel, group), grid=(heads,), in...]
    ppermute x1 -> x2, starting transfers between devices: 16.2 us -> 8.82 us  [from_behind(): lax.ppermute(value, axis, [(source, source + steps) for source in range(l...]
    dot_general x11 -> x0, matrix products: 5.52 us -> none  [the longest x2 1.87 us: attend_back(): jnp.einsum('blhe,bmhe->bhlm', grad_out, values, preferred_element_type=jn...]
    convert_element_type x4 -> x0, local copies, waits for them, and re-layouts: 2.76 us -> none  [the longest x1 0.88 us: attend_back(): grad_query.astype(jnp.bfloat16)]
  transfers between devices with their start and end apart: 5 -> 3, of which waited for: 5 -> 3; matrix products, arithmetic and copies ran while one was open for 6% -> 1% of each run, Pallas kernels for 0% -> 4%
where the time goes in v1:
time: 134 us; the launch traced here: 133 us
  waiting for transfers between devices  53 us (40%)
  blocking collectives  51.9 us (39%)
  starting transfers between devices  12.7 us (9%)
  Pallas kernels  9.74 us (7%)
  other arithmetic  4.48 us (3%)
    all_to_all x1, blocking collectives, on_device(): lax.all_to_all(sent, 'seq', split_axis=0, concat_axis=0, tiled=True)  51.9 us
    ppermute x2, waiting for transfers between devices, from_behind(): lax.ppermute(value, axis, [(source, source + steps) for source in range(l...  41.3 us
    all_to_all x1, waiting for transfers between devices, on_device(): lax.all_to_all(col_sent, 'seq', split_axis=0, concat_axis=0, tiled=True)  11.8 us
    pallas_call x2, Pallas kernels, attend_back(): pl.pallas_call(functools.partial(attend_kernel, group), grid=(heads,), in...  9.74 us
    ppermute x2, starting transfers between devices, from_behind(): lax.ppermute(value, axis, [(source, source + steps) for source in range(l...  8.82 us
    all_to_all x1, starting transfers between devices, on_device(): lax.all_to_all(col_sent, 'seq', split_axis=0, concat_axis=0, tiled=True)  3.91 us
  transfers between devices with their start and end apart: 3, of which 3 were waited for; matrix products, arithmetic and copies ran while one was open for 1% of the time, Pallas kernels for 4%

profile of v1, /device:TPU:1, one launch (start us, length us, event | category | flops | bytes accessed | tf_op | source)
XLA Modules:
  0.0 133.2 jit_solution(13695786584899481396)
XLA Ops:
  0.0 1.3 pad_maximum_fusion
  1.3 51.9 %all_to_all.10 = bf16[32,8,2048]{2,1,0:T(8,128)(2,1)} all-to-all(bf16[32,8,2048]{2,1,0:T(8,128)(2,1)S(1)} %pad_maximum_fusion), channel_id=1, replica_groups=mesh['section'=16,'seq'=32] {'seq'}, dimensions={0} | all-to-all | bytes 2097152 | tf_op jit(solution)/shard_map/all_to_all | solution.py:92
  53.1 4.9 %shard_map.83 = (bf16[256,512]{1,0:T(8,128)(2,1)}, bf16[256,512]{1,0:T(8,128)(2,1)}, bf16[256,512]{1,0:T(8,128)(2,1)}) custom-call(bf16[256,2048]{1,0:T(8,128)(2,1)} %bitcast.13, bf16[256,2048]{1,0:T(8,128)(2,1)} %bitcast.14, bf16[256,2048]{1,0:T(8,128)(2,1)} %bitcast.15, bf16[256,2048]{1,0:T(8,128)(2,1)} %bitcast.16), custom_call_target="tpu_custom_call" | custom-call | flops 335544320 | bytes 1835008 | tf_op jit(solution)/shard_map/pallas_call | solution.py:72
  58.0 2.0 %maximum_bitcast_fusion = bf16[32,8,1536]{2,1,0:T(8,128)(2,1)} fusion(bf16[256,512]{1,0:T(8,128)(2,1)} %get-tuple-element.16, bf16[256,512]{1,0:T(8,128)(2,1)} %get-tuple-element.15, bf16[256,512]{1,0:T(8,128)(2,1)} %get-tuple-element.14), kind=kLoop, calls=%fused_computation.2 | loop fusion | flops 2359296 | bytes 1572864 | tf_op jit(solution)/shard_map/reshape | solution.py:103
  60.1 3.9 %all-to-all-start.1 = ((bf16[32,8,1536]{2,1,0:T(8,128)(2,1)}), bf16[32,8,1536]{2,1,0:T(8,128)(2,1)S(1)}, u32[]{:S(2)}, u32[]{:S(2)}) async-start(bf16[32,8,1536]{2,1,0:T(8,128)(2,1)} %maximum_bitcast_fusion), calls=%async_computation.1 | async-start | bytes 1572864 | tf_op jit(solution)/shard_map/all_to_all | solution.py:104
  64.0 4.8 %shard_map.82 = (bf16[256,512]{1,0:T(8,128)(2,1)}, bf16[256,512]{1,0:T(8,128)(2,1)}, bf16[256,512]{1,0:T(8,128)(2,1)}) custom-call(bf16[256,512]{1,0:T(8,128)(2,1)} %bitcast.22, bf16[256,512]{1,0:T(8,128)(2,1)} %bitcast.23, bf16[256,512]{1,0:T(8,128)(2,1)} %bitcast.24, bf16[256,512]{1,0:T(8,128)(2,1)} %bitcast.25), custom_call_target="tpu_custom_call" | custom-call | flops 335544320 | bytes 1835008 | tf_op jit(solution)/shard_map/pallas_call | solution.py:72
  68.8 1.2 pad_maximum_fusion.1
  70.0 3.9 %collective-permute-start = (bf16[256,1536]{1,0:T(8,128)(2,1)S(1)}, bf16[256,1536]{1,0:T(8,128)(2,1)S(1)}, u32[]{:S(2)}, u32[]{:S(2)}) collective-permute-start(bf16[256,1536]{1,0:T(8,128)(2,1)S(1)} %pad_maximum_fusion.1), channel_id=1, source_target_pairs={{32,0},{64,32},{96,64},{128,96},{160,128},{192,160},{224,192},{256... | collective-permute-start | bytes 2359304 | tf_op jit(solution)/shard_map/ppermute | solution.py:19
  73.9 11.8 %all-to-all-done.1 = bf16[32,8,1536]{2,1,0:T(8,128)(2,1)S(1)} async-done(((bf16[32,8,1536]{2,1,0:T(8,128)(2,1)}), bf16[32,8,1536]{2,1,0:T(8,128)(2,1)S(1)}, u32[]{:S(2)}, u32[]{:S(2)}) %all-to-all-start.1) | async-done | bytes 786464 | tf_op jit(solution)/shard_map/all_to_all | solution.py:104
  85.6 4.9 %collective-permute-start.1 = (bf16[256,1536]{1,0:T(8,128)(2,1)S(1)}, bf16[256,1536]{1,0:T(8,128)(2,1)S(1)}, u32[]{:S(2)}, u32[]{:S(2)}) collective-permute-start(bf16[256,1536]{1,0:T(8,128)(2,1)S(1)} %bitcast.17), channel_id=1, source_target_pairs={{32,0},{64,32},{96,64},{128,96},{160,128},{192,160},{224,192},{256... | collective-permute-start | bytes 2359304 | tf_op jit(solution)/shard_map/ppermute | solution.py:19
  90.6 30.2 %collective-permute-done = bf16[256,1536]{1,0:T(8,128)(2,1)S(1)} collective-permute-done((bf16[256,1536]{1,0:T(8,128)(2,1)S(1)}, bf16[256,1536]{1,0:T(8,128)(2,1)S(1)}, u32[]{:S(2)}, u32[]{:S(2)}) %collective-permute-start) | collective-permute-done | bytes 786464 | tf_op jit(solution)/shard_map/ppermute | solution.py:19
  120.8 11.1 %collective-permute-done.1 = bf16[256,1536]{1,0:T(8,128)(2,1)S(1)} collective-permute-done((bf16[256,1536]{1,0:T(8,128)(2,1)S(1)}, bf16[256,1536]{1,0:T(8,128)(2,1)S(1)}, u32[]{:S(2)}, u32[]{:S(2)}) %collective-permute-start.1) | collective-permute-done | bytes 786464 | tf_op jit(solution)/shard_map/ppermute | solution.py:19
  132.1 0.0 copy-start
  132.1 1.1 copy-done
  (6 shorter events, 0.1 us)
Async XLA Ops:
  60.1 25.6 %all-to-all-start.1 = ((bf16[32,8,1536]{2,1,0:T(8,128)(2,1)}), bf16[32,8,1536]{2,1,0:T(8,128)(2,1)S(1)}, u32[]{:S(2)}, u32[]{:S(2)}) async-start(bf16[32,8,1536]{2,1,0:T(8,128)(2,1)} %maximum_bitcast_fusion), calls=%async_computation.1 | async-start | bytes 1572864 | tf_op jit(solution)/shard_map/all_to_all | solution.py:104
  70.0 50.8 %collective-permute-start = (bf16[256,1536]{1,0:T(8,128)(2,1)S(1)}, bf16[256,1536]{1,0:T(8,128)(2,1)S(1)}, u32[]{:S(2)}, u32[]{:S(2)}) collective-permute-start(bf16[256,1536]{1,0:T(8,128)(2,1)S(1)} %pad_maximum_fusion.1), channel_id=1, source_target_pairs={{32,0},{64,32},{96,64},{128,96},{160,128},{192,160},{224,192},{256... | collective-permute-start | bytes 2359304 | tf_op jit(solution)/shard_map/ppermute | solution.py:19
  85.6 46.2 %collective-permute-start.1 = (bf16[256,1536]{1,0:T(8,128)(2,1)S(1)}, bf16[256,1536]{1,0:T(8,128)(2,1)S(1)}, u32[]{:S(2)}, u32[]{:S(2)}) collective-permute-start(bf16[256,1536]{1,0:T(8,128)(2,1)S(1)} %bitcast.17), channel_id=1, source_target_pairs={{32,0},{64,32},{96,64},{128,96},{160,128},{192,160},{224,192},{256... | collective-permute-start | bytes 2359304 | tf_op jit(solution)/shard_map/ppermute | solution.py:19
  132.1 1.1 copy-start

commit v2 on v1

v2 whole, which is shorter than its diff:
```python
import functools

import jax
import jax.numpy as jnp
from jax import lax
from jax.experimental import pallas as pl
from jax.experimental.pallas import tpu as pltpu
from jax.sharding import PartitionSpec as P

H_ROW = 4
H_COL = 4
HD = 128
COLS = 256
LOG2E = 1.4426950408889634


def from_behind(value, axis, steps):
    count = lax.axis_size(axis)
    leading, last = (max(0, -steps), min(count, count - steps))
    return lax.ppermute(value, axis, [(source, source + steps) for source in range(leading, last)])


def dot(a, b, over_a, over_b):
    dims = (((over_a,), (over_b,)), ((), ()))
    return lax.dot_general(a, b, dims, preferred_element_type=jnp.float32)


def head_back(queries, keys, values, grad_out, allowed):
    scaling = HD ** (-0.5)
    scores = jnp.where(allowed, dot(keys, queries, 1, 1), -1e30)
    largest = jnp.max(scores, axis=0, keepdims=True)
    weights = jnp.exp2((scores - largest) * (scaling * LOG2E))
    probability = weights * (1.0 / jnp.sum(weights, axis=0, keepdims=True))
    prob_low = probability.astype(jnp.bfloat16)
    grad_probs = dot(values, grad_out, 1, 1)
    inner_sum = jnp.sum(prob_low.astype(jnp.float32) * grad_probs, axis=0, keepdims=True)
    grad_low = (probability * ((grad_probs - inner_sum) * scaling)).astype(jnp.bfloat16)
    return (
        dot(grad_low, keys, 0, 0).astype(jnp.bfloat16),
        dot(grad_low, queries, 1, 0).astype(jnp.bfloat16),
        dot(prob_low, grad_out, 1, 0).astype(jnp.bfloat16),
    )


def attend_kernel(group, heads, places, *refs):
    ins, out_ref = refs[:-1], refs[-1]
    tokens = out_ref.shape[0]
    key_at = lax.broadcasted_iota(jnp.int32, (tokens, tokens), 0)
    query_at = lax.broadcasted_iota(jnp.int32, (tokens, tokens), 1)
    allowed = query_at >= key_at
    if group > 1:
        allowed = allowed & (lax.rem(query_at, group) == lax.rem(key_at, group))
    for h in range(heads):
        taken = [ins[i][:, (at + h) * HD : (at + h + 1) * HD] for i, at in places]
        for i, grad in enumerate(head_back(*taken, allowed)):
            at = i * heads + h
            out_ref[:, at * HD : (at + 1) * HD] = grad


def attend_back(group, heads, operands, places):
    tokens = operands[0].shape[0]
    width = heads * HD
    pairs = heads * tokens * tokens
    return pl.pallas_call(
        functools.partial(attend_kernel, group, heads, places),
        in_specs=[pl.BlockSpec(memory_space=pltpu.VMEM)] * len(operands),
        out_specs=pl.BlockSpec(memory_space=pltpu.VMEM),
        out_shape=jax.ShapeDtypeStruct((tokens, 3 * width), jnp.bfloat16),
        compiler_params=pltpu.CompilerParams(vmem_limit_bytes=24 * 1024 * 1024),
        cost_estimate=pl.CostEstimate(
            flops=10 * pairs * HD, bytes_accessed=14 * tokens * width, transcendentals=pairs
        ),
    )(*operands)


def on_device(
    query_row, key_row, value_row, cotangent_row, query_col, key_col, value_col, cotangent_col
):
    tokens_dev, width = query_row.shape[1:]
    groups = lax.axis_size("seq")
    col_group = COLS // groups
    sent = jnp.concatenate([query_col[0], key_col[0], value_col[0], cotangent_col[0]], axis=-1)
    sent = sent.reshape(groups, col_group, 4 * width)
    arrived = lax.all_to_all(sent, "seq", split_axis=0, concat_axis=0, tiled=True)
    arrived = arrived.reshape(groups * col_group, 4 * width)

    row_part = attend_back(
        1,
        H_ROW,
        (query_row[0], key_row[0], value_row[0], cotangent_row[0]),
        ((0, 0), (1, 0), (2, 0), (3, 0)),
    )
    row_pack = from_behind(row_part, "section", -1)
    arrived, row_pack = lax.optimization_barrier((arrived, row_pack))

    col_part = attend_back(
        col_group, H_COL, (arrived,), ((0, 0), (0, H_COL), (0, 2 * H_COL), (0, 3 * H_COL))
    )
    col_sent = col_part.reshape(groups, col_group, 3 * width)
    col_pack = lax.all_to_all(col_sent, "seq", split_axis=0, concat_axis=0, tiled=True)
    col_pack = from_behind(col_pack.reshape(tokens_dev, 3 * width), "section", -1)
    pieces = []
    for i in range(3):
        pieces += [row_pack[:, i * width : (i + 1) * width], col_pack[:, i * width : (i + 1) * width]]
    return jnp.concatenate(pieces, axis=-1)[None]


def solution(mesh):
    return jax.shard_map(
        on_device,
        mesh=mesh,
        in_specs=(P("section", "seq", None),) * 8,
        out_specs=P("section", "seq", None),
        check_vma=False,
    )
```

time: 134 us -> 160 us (1.19)
  waiting for transfers between devices: 53 us -> 78.6 us
  starting transfers between devices: 12.7 us -> 26 us
  Pallas kernels: 9.74 us -> 3.7 us
  blocking collectives: 51.9 us -> 48 us
  other arithmetic: 4.48 us -> 2.28 us
    ppermute x2, waiting for transfers between devices: 41.3 us -> 78.6 us  [from_behind(): lax.ppermute(value, axis, [(source, source + steps) for source in range(l...]
    all_to_all x1, starting transfers between devices: 3.91 us -> 21.3 us  [on_device(): lax.all_to_all(sent, 'seq', split_axis=0, concat_axis=0, tiled=True)]
    all_to_all x1, waiting for transfers between devices: 11.8 us -> 0.01 us  [on_device(): lax.all_to_all(sent, 'seq', split_axis=0, concat_axis=0, tiled=True)]
    pallas_call x2, Pallas kernels: 9.74 us -> 3.7 us  [attend_back(): pl.pallas_call(functools.partial(attend_kernel, group, heads, places), in...]
    ppermute x2, starting transfers between devices: 8.82 us -> 4.77 us  [from_behind(): lax.ppermute(value, axis, [(source, source + steps) for source in range(l...]
    all_to_all x1, blocking collectives: 51.9 us -> 48 us  [on_device(): lax.all_to_all(col_sent, 'seq', split_axis=0, concat_axis=0, tiled=True)]
    reshape x1 -> x0, other arithmetic: 2.04 us -> none  [on_device(): jnp.concatenate(col_part, axis=-1).reshape(groups, col_group, 3 * width)]
  transfers between devices with their start and end apart: 3 -> 3, of which waited for: 3 -> 2; matrix products, arithmetic and copies ran while one was open for 1% -> 0% of each run, Pallas kernels for 4% -> 1%
where the time goes in v2:
time: 160 us
  waiting for transfers between devices  78.6 us (49%)
  blocking collectives  48 us (30%)
  starting transfers between devices  26 us (16%)
  Pallas kernels  3.7 us (2%)
  other arithmetic  2.28 us (1%)
    ppermute x2, waiting for transfers between devices, from_behind(): lax.ppermute(value, axis, [(source, source + steps) for source in range(l...  78.6 us
    all_to_all x1, blocking collectives, on_device(): lax.all_to_all(col_sent, 'seq', split_axis=0, concat_axis=0, tiled=True)  48 us
    all_to_all x1, starting transfers between devices, on_device(): lax.all_to_all(sent, 'seq', split_axis=0, concat_axis=0, tiled=True)  21.3 us
    ppermute x2, starting transfers between devices, from_behind(): lax.ppermute(value, axis, [(source, source + steps) for source in range(l...  4.77 us
    pallas_call x2, Pallas kernels, attend_back(): pl.pallas_call(functools.partial(attend_kernel, group, heads, places), in...  3.7 us
  transfers between devices with their start and end apart: 3, of which 2 were waited for; matrix products, arithmetic and copies ran while one was open for 0% of the time, Pallas kernels for 1%

profile of v2, /device:TPU:1, one launch (start us, length us, event | category | flops | bytes accessed | tf_op | source)
XLA Modules:
  0.0 160.0 jit_solution(2537009995069656632)
XLA Ops:
  0.0 2.3 %pad_maximum_fusion = bf16[32,8,2048]{2,1,0:T(8,128)(2,1)} fusion(bf16[32,8,512]{2,1,0:T(8,128)(2,1)} %bitcast.19, bf16[32,8,512]{2,1,0:T(8,128)(2,1)} %bitcast.20, bf16[32,8,512]{2,1,0:T(8,128)(2,1)} %bitcast.21, bf16[32,8,512]{2,1,0:T(8,128)(2,1)} %bitcast.22), kind=kLoop, calls=%fused_computation | loop fusion | flops 4194304 | bytes 2097152 | tf_op jit(solution)/shard_map/concatenate | solution.py:82
  2.3 0.0 copy-start
  2.3 0.0 copy-start.1
  2.3 0.0 copy-start.2
  2.3 0.0 copy-start.3
  2.3 21.3 %all-to-all-start = ((bf16[32,8,2048]{2,1,0:T(8,128)(2,1)}), bf16[32,8,2048]{2,1,0:T(8,128)(2,1)S(1)}, u32[]{:S(2)}, u32[]{:S(2)}) async-start(bf16[32,8,2048]{2,1,0:T(8,128)(2,1)} %pad_maximum_fusion), calls=%async_computation | async-start | bytes 2097152 | tf_op jit(solution)/shard_map/all_to_all | solution.py:84
  23.6 0.0 copy-done
  23.6 0.0 copy-done.1
  23.6 0.0 copy-done.2
  23.6 0.0 copy-done.3
  23.6 1.8 %shard_map.82 = bf16[256,1536]{1,0:T(8,128)(2,1)S(1)} custom-call(bf16[256,512]{1,0:T(8,128)(2,1)S(1)} %bitcast.14, bf16[256,512]{1,0:T(8,128)(2,1)S(1)} %bitcast.15, bf16[256,512]{1,0:T(8,128)(2,1)S(1)} %bitcast.16, bf16[256,512]{1,0:T(8,128)(2,1)S(1)} %bitcast.17), custom_call_target="tpu_custom_call" | custom-call | flops 335544320 | bytes 1835008 | tf_op jit(solution)/shard_map/pallas_call | solution.py:64
  25.5 2.9 %collective-permute-start = (bf16[256,1536]{1,0:T(8,128)(2,1)S(1)}, bf16[256,1536]{1,0:T(8,128)(2,1)S(1)}, u32[]{:S(2)}, u32[]{:S(2)}) collective-permute-start(bf16[256,1536]{1,0:T(8,128)(2,1)S(1)} %shard_map.82), channel_id=1, source_target_pairs={{32,0},{64,32},{96,64},{128,96},{160,128},{192,160},{224,192},{256... | collective-permute-start | bytes 2359304 | tf_op jit(solution)/shard_map/ppermute | solution.py:20
  28.3 50.6 %collective-permute-done = bf16[256,1536]{1,0:T(8,128)(2,1)S(1)} collective-permute-done((bf16[256,1536]{1,0:T(8,128)(2,1)S(1)}, bf16[256,1536]{1,0:T(8,128)(2,1)S(1)}, u32[]{:S(2)}, u32[]{:S(2)}) %collective-permute-start) | collective-permute-done | bytes 786464 | tf_op jit(solution)/shard_map/ppermute | solution.py:20
  79.0 0.0 all-to-all-done
  79.0 1.9 %shard_map.83 = bf16[256,1536]{1,0:T(8,128)(2,1)S(1)} custom-call(bf16[256,2048]{1,0:T(8,128)(2,1)S(1)} %bitcast.12), custom_call_target="tpu_custom_call" | custom-call | flops 335544320 | bytes 1835008 | tf_op jit(solution)/shard_map/pallas_call | solution.py:64
  80.8 48.0 %all_to_all.10 = bf16[32,8,1536]{2,1,0:T(8,128)(2,1)S(1)} all-to-all(bf16[32,8,1536]{2,1,0:T(8,128)(2,1)S(1)} %bitcast.13), channel_id=1, replica_groups=mesh['section'=16,'seq'=32] {'seq'}, dimensions={0} | all-to-all | bytes 1572864 | tf_op jit(solution)/shard_map/all_to_all | solution.py:100
  128.8 1.9 %collective-permute-start.1 = (bf16[256,1536]{1,0:T(8,128)(2,1)S(1)}, bf16[256,1536]{1,0:T(8,128)(2,1)S(1)}, u32[]{:S(2)}, u32[]{:S(2)}) collective-permute-start(bf16[256,1536]{1,0:T(8,128)(2,1)S(1)} %bitcast.18), channel_id=1, source_target_pairs={{32,0},{64,32},{96,64},{128,96},{160,128},{192,160},{224,192},{256... | collective-permute-start | bytes 2359304 | tf_op jit(solution)/shard_map/ppermute | solution.py:20
  130.8 27.9 %collective-permute-done.1 = bf16[256,1536]{1,0:T(8,128)(2,1)S(1)} collective-permute-done((bf16[256,1536]{1,0:T(8,128)(2,1)S(1)}, bf16[256,1536]{1,0:T(8,128)(2,1)S(1)}, u32[]{:S(2)}, u32[]{:S(2)}) %collective-permute-start.1) | collective-permute-done | bytes 786464 | tf_op jit(solution)/shard_map/ppermute | solution.py:20
  158.9 0.0 copy-start.4
  158.9 1.1 copy-done.4
  (6 shorter events, 0.1 us)
Async XLA Ops:
  2.3 21.3 %copy-start = (bf16[1,256,512]{2,1,0:T(8,128)(2,1)S(1)}, bf16[1,256,512]{2,1,0:T(8,128)(2,1)}, u32[]{:S(2)}) copy-start(bf16[1,256,512]{2,1,0:T(8,128)(2,1)} %param.8) | copy-start | bytes 786436
  2.3 21.3 %copy-start.1 = (bf16[1,256,512]{2,1,0:T(8,128)(2,1)S(1)}, bf16[1,256,512]{2,1,0:T(8,128)(2,1)}, u32[]{:S(2)}) copy-start(bf16[1,256,512]{2,1,0:T(8,128)(2,1)} %param.9) | copy-start | bytes 786436
  2.3 21.3 %copy-start.2 = (bf16[1,256,512]{2,1,0:T(8,128)(2,1)S(1)}, bf16[1,256,512]{2,1,0:T(8,128)(2,1)}, u32[]{:S(2)}) copy-start(bf16[1,256,512]{2,1,0:T(8,128)(2,1)} %param.10) | copy-start | bytes 786436
  2.3 21.3 %copy-start.3 = (bf16[1,256,512]{2,1,0:T(8,128)(2,1)S(1)}, bf16[1,256,512]{2,1,0:T(8,128)(2,1)}, u32[]{:S(2)}) copy-start(bf16[1,256,512]{2,1,0:T(8,128)(2,1)} %param.11) | copy-start | bytes 786436
  2.3 76.7 %all-to-all-start = ((bf16[32,8,2048]{2,1,0:T(8,128)(2,1)}), bf16[32,8,2048]{2,1,0:T(8,128)(2,1)S(1)}, u32[]{:S(2)}, u32[]{:S(2)}) async-start(bf16[32,8,2048]{2,1,0:T(8,128)(2,1)} %pad_maximum_fusion), calls=%async_computation | async-start | bytes 2097152 | tf_op jit(solution)/shard_map/all_to_all | solution.py:84
  25.5 53.5 %collective-permute-start = (bf16[256,1536]{1,0:T(8,128)(2,1)S(1)}, bf16[256,1536]{1,0:T(8,128)(2,1)S(1)}, u32[]{:S(2)}, u32[]{:S(2)}) collective-permute-start(bf16[256,1536]{1,0:T(8,128)(2,1)S(1)} %shard_map.82), channel_id=1, source_target_pairs={{32,0},{64,32},{96,64},{128,96},{160,128},{192,160},{224,192},{256... | collective-permute-start | bytes 2359304 | tf_op jit(solution)/shard_map/ppermute | solution.py:20
  128.8 29.9 %collective-permute-start.1 = (bf16[256,1536]{1,0:T(8,128)(2,1)S(1)}, bf16[256,1536]{1,0:T(8,128)(2,1)S(1)}, u32[]{:S(2)}, u32[]{:S(2)}) collective-permute-start(bf16[256,1536]{1,0:T(8,128)(2,1)S(1)} %bitcast.18), channel_id=1, source_target_pairs={{32,0},{64,32},{96,64},{128,96},{160,128},{192,160},{224,192},{256... | collective-permute-start | bytes 2359304 | tf_op jit(solution)/shard_map/ppermute | solution.py:20
  158.9 1.1 copy-start.4

commit v3 on v2

v3 whole, which is shorter than its diff:
```python
import functools

import jax
import jax.numpy as jnp
from jax import lax
from jax.experimental import pallas as pl
from jax.experimental.pallas import tpu as pltpu
from jax.sharding import PartitionSpec as P

H_ROW = 4
H_COL = 4
HD = 128
COLS = 256
LOG2E = 1.4426950408889634
CHUNKS = 2
AXES = ("section", "seq")
VMEM = pl.BlockSpec(memory_space=pltpu.VMEM)
SMEM = pl.BlockSpec(memory_space=pltpu.SMEM)
LEFT = pl.BlockSpec(memory_space=pl.ANY)
PARAMS = pltpu.CompilerParams(vmem_limit_bytes=24 * 1024 * 1024)


def shifted(value, steps, flip, first):
    sections, seqs = lax.axis_size("section"), lax.axis_size("seq")
    pairs = [
        (s * seqs + q, (s - steps) * seqs + (q ^ flip))
        for s in range(first, sections)
        for q in range(seqs)
    ]
    return lax.ppermute(value, AXES, pairs)


def same_half(value):
    seqs = lax.axis_size("seq")
    groups = [[q for q in range(seqs) if q % 2 == half] for half in range(2)]
    return lax.all_to_all(value, "seq", 0, 0, axis_index_groups=groups, tiled=True)


def dot(a, b, over_a, over_b):
    dims = (((over_a,), (over_b,)), ((), ()))
    return lax.dot_general(a, b, dims, preferred_element_type=jnp.float32)


def head_back(queries, keys, values, grad_out, allowed):
    scaling = HD ** (-0.5)
    scores = jnp.where(allowed, dot(keys, queries, 1, 1), -1e30)
    largest = jnp.max(scores, axis=0, keepdims=True)
    weights = jnp.exp2((scores - largest) * (scaling * LOG2E))
    probability = weights * (1.0 / jnp.sum(weights, axis=0, keepdims=True))
    prob_low = probability.astype(jnp.bfloat16)
    grad_probs = dot(values, grad_out, 1, 1)
    inner_sum = jnp.sum(prob_low.astype(jnp.float32) * grad_probs, axis=0, keepdims=True)
    grad_low = (probability * ((grad_probs - inner_sum) * scaling)).astype(jnp.bfloat16)
    return (
        dot(grad_low, keys, 0, 0).astype(jnp.bfloat16),
        dot(grad_low, queries, 1, 0).astype(jnp.bfloat16),
        dot(prob_low, grad_out, 1, 0).astype(jnp.bfloat16),
    )


def cost(heads, tokens):
    pairs = heads * tokens * tokens
    return pl.CostEstimate(
        flops=10 * pairs * HD, bytes_accessed=14 * tokens * heads * HD, transcendentals=pairs
    )


def row_kernel(q_ref, k_ref, v_ref, g_ref, out_ref):
    tokens = out_ref.shape[0]
    key_at = lax.broadcasted_iota(jnp.int32, (tokens, tokens), 0)
    query_at = lax.broadcasted_iota(jnp.int32, (tokens, tokens), 1)
    allowed = query_at >= key_at
    for h in range(H_ROW):
        lanes = slice(h * HD, (h + 1) * HD)
        taken = [ref[:, lanes] for ref in (q_ref, k_ref, v_ref, g_ref)]
        for i, grad in enumerate(head_back(*taken, allowed)):
            at = i * H_ROW + h
            out_ref[:, at * HD : (at + 1) * HD] = grad


def row_grads(operands):
    tokens = operands[0].shape[0]
    return pl.pallas_call(
        row_kernel,
        in_specs=[VMEM] * 4,
        out_specs=VMEM,
        out_shape=jax.ShapeDtypeStruct((tokens, 3 * H_ROW * HD), jnp.bfloat16),
        compiler_params=PARAMS,
        cost_estimate=cost(H_ROW, tokens),
    )(*operands)


def pack_kernel(start, half_ref, q_ref, k_ref, v_ref, g_ref, *refs):
    out_ref = refs[-1]
    group = out_ref.shape[1] // 2
    width = out_ref.shape[2] // 4
    for i, ref in enumerate((q_ref, k_ref, v_ref, g_ref)):
        for part in range(2):
            first = pl.multiple_of((half_ref[0] ^ part) * group, group)
            out_ref[:, part * group : (part + 1) * group, i * width : (i + 1) * width] = ref[
                :, pl.ds(first, group), start : start + width
            ]


def pack(half, operands, chunk, after):
    rows, columns, lanes = operands[0].shape
    width = lanes // CHUNKS
    return pl.pallas_call(
        functools.partial(pack_kernel, chunk * width),
        in_specs=[SMEM] + [VMEM] * 4 + [LEFT] * len(after),
        out_specs=VMEM,
        out_shape=jax.ShapeDtypeStruct((rows, columns, 4 * width), jnp.bfloat16),
        compiler_params=PARAMS,
        cost_estimate=pl.CostEstimate(
            flops=0, bytes_accessed=4 * rows * columns * 4 * width, transcendentals=0
        ),
    )(half, *operands, *after)


def col_kernel(half_ref, own_ref, far_ref, *refs):
    own_out, far_out = refs[-2:]
    rows, group, lanes = far_ref.shape
    width = lanes // 4
    heads = width // HD
    tokens = rows * group

    def place(dim):
        at = lax.broadcasted_iota(jnp.int32, (2 * tokens, 2 * tokens), dim)
        far = (at >= tokens).astype(jnp.int32)
        grid_row = 2 * ((at - far * tokens) // group) + (half_ref[0] ^ far)
        return grid_row, lax.rem(at, group)

    key_row, key_col = place(0)
    query_row, query_col = place(1)
    allowed = (query_row >= key_row) & (query_col == key_col)
    for h in range(heads):
        taken = []
        for i in range(4):
            lane = slice(i * width + h * HD, i * width + (h + 1) * HD)
            taken.append(
                jnp.concatenate(
                    [
                        own_ref[:, :group, lane].reshape(tokens, HD),
                        far_ref[:, :, lane].reshape(tokens, HD),
                    ],
                    axis=0,
                )
            )
        for i, grad in enumerate(head_back(*taken, allowed)):
            lane = slice(i * width + h * HD, i * width + (h + 1) * HD)
            own_out[:, :, lane] = grad[:tokens].reshape(rows, group, HD)
            far_out[:, :, lane] = grad[tokens:].reshape(rows, group, HD)


def col_grads(half, own, far, after):
    rows, group, lanes = far.shape
    result = jax.ShapeDtypeStruct((rows, group, 3 * lanes // 4), jnp.bfloat16)
    return pl.pallas_call(
        col_kernel,
        in_specs=[SMEM, VMEM, VMEM] + [LEFT] * len(after),
        out_specs=[VMEM, VMEM],
        out_shape=[result, result],
        compiler_params=PARAMS,
        cost_estimate=cost(lanes // 4 // HD, 2 * rows * group),
    )(half, own, far, *after)


def join_kernel(own_ref, far_ref, *refs):
    group = own_ref.shape[1]
    refs[-1][:, :group, :] = own_ref[...]
    refs[-1][:, group:, :] = far_ref[...]


def join(own, far, after):
    rows, group, lanes = own.shape
    return pl.pallas_call(
        join_kernel,
        in_specs=[VMEM, VMEM] + [LEFT] * len(after),
        out_specs=VMEM,
        out_shape=jax.ShapeDtypeStruct((rows, 2 * group, lanes), jnp.bfloat16),
        compiler_params=PARAMS,
        cost_estimate=pl.CostEstimate(
            flops=0, bytes_accessed=8 * rows * group * lanes, transcendentals=0
        ),
    )(own, far, *after)


def unpack_kernel(half_ref, row_ref, *refs):
    parts, out_ref = refs[:-1], refs[-1]
    group = out_ref.shape[1] // 2
    wide = out_ref.shape[2] // 6
    width = wide // CHUNKS
    for i in range(3):
        out_ref[:, :, 2 * i * wide : (2 * i + 1) * wide] = row_ref[:, :, i * wide : (i + 1) * wide]
        for c, ref in enumerate(parts):
            lane = (2 * i + 1) * wide + c * width
            for part in range(2):
                first = pl.multiple_of((half_ref[0] ^ part) * group, group)
                out_ref[:, part * group : (part + 1) * group, lane : lane + width] = ref[
                    :, pl.ds(first, group), i * width : (i + 1) * width
                ]


def unpack(half, row_part, parts):
    rows, columns, lanes = row_part.shape
    return pl.pallas_call(
        unpack_kernel,
        in_specs=[SMEM] + [VMEM] * (1 + len(parts)),
        out_specs=VMEM,
        out_shape=jax.ShapeDtypeStruct((rows, columns, 2 * lanes), jnp.bfloat16),
        compiler_params=PARAMS,
        cost_estimate=pl.CostEstimate(
            flops=0, bytes_accessed=8 * rows * columns * lanes, transcendentals=0
        ),
    )(half, row_part, *parts)


def on_device(
    query_row, key_row, value_row, cotangent_row, query_col, key_col, value_col, cotangent_col
):
    tokens_dev, width = query_row.shape[1:]
    places = lax.axis_size("seq") // 2
    columns = COLS // places
    group = columns // 2
    half = lax.rem(lax.axis_index("seq"), 2).astype(jnp.int32).reshape(1)
    col_in = [
        block[0].reshape(places, columns, width)
        for block in (query_col, key_col, value_col, cotangent_col)
    ]

    row_part = row_grads((query_row[0], key_row[0], value_row[0], cotangent_row[0]))
    near = [same_half(pack(half, col_in, 0, ()))]
    sent = [near[0][:, group:]]
    far = [shifted(sent[0], 0, 1, 1)]
    row_pack = shifted(row_part, 1, 0, 1)
    near.append(same_half(pack(half, col_in, 1, (row_part,))))
    sent.append(near[1][:, group:])
    far.append(shifted(sent[1], 0, 1, 1))
    own, distant = col_grads(half, near[0], far[0], (sent[1],))
    back = [(shifted(distant, 1, 1, 1), shifted(own, 1, 0, 1))]
    own, distant = col_grads(half, near[1], far[1], ())
    back.append((shifted(distant, 1, 1, 1), shifted(own, 1, 0, 1)))
    parts = [same_half(join(back[0][1], back[0][0], (own,)))]
    parts.append(same_half(join(back[1][1], back[1][0], ())))
    result = unpack(half, row_pack.reshape(places, columns, 3 * width), parts)
    return result.reshape(1, tokens_dev, 6 * width)


def solution(mesh):
    return jax.shard_map(
        on_device,
        mesh=mesh,
        in_specs=(P("section", "seq", None),) * 8,
        out_specs=P("section", "seq", None),
        check_vma=False,
    )
```

time: 160 us -> 161 us (level)
  blocking collectives: 48 us -> 0 us
  starting transfers between devices: 26 us -> 61.6 us
  waiting for transfers between devices: 78.6 us -> 85.6 us
  Pallas kernels: 3.7 us -> 8.63 us
  local copies, waits for them, and re-layouts: 1.3 us -> 3.87 us
  other arithmetic: 2.28 us -> 0 us
    all_to_all x1 -> x0, blocking collectives: 48 us -> none  [on_device(): lax.all_to_all(col_sent, 'seq', split_axis=0, concat_axis=0, tiled=True)]
    ppermute x2 -> x7, starting transfers between devices: 4.77 us -> 37 us  [shifted(): return lax.ppermute(value, AXES, pairs)]
    all_to_all x1 -> x4, waiting for transfers between devices: 0.01 us -> 16 us  [same_half(): lax.all_to_all(value, 'seq', 0, 0, axis_index_groups=groups, tiled=True)]
    ppermute x2 -> x7, waiting for transfers between devices: 78.6 us -> 69.6 us  [shifted(): return lax.ppermute(value, AXES, pairs)]
    pallas_call x2 -> x8, Pallas kernels: 3.7 us -> 8.63 us  [the longest x2 2.18 us: col_grads(): pl.pallas_call(col_kernel, in_specs=[SMEM, VMEM, VMEM] + [LEFT] * len(aft...]
    all_to_all x1 -> x4, starting transfers between devices: 21.3 us -> 24.6 us  [same_half(): lax.all_to_all(value, 'seq', 0, 0, axis_index_groups=groups, tiled=True)]
    unnamed x15 -> x24, local copies, waits for them, and re-layouts: 1.28 us -> 3.83 us
    concatenate x1 -> x0, other arithmetic: 2.28 us -> none  [on_device(): jnp.concatenate([query_col[0], key_col[0], value_col[0], cotangent_col[0]...]
  transfers between devices with their start and end apart: 3 -> 11, of which waited for: 2 -> 6; matrix products, arithmetic and copies ran while one was open for 0% -> 0% of each run, Pallas kernels for 1% -> 4%
where the time goes in v3:
time: 161 us; the launch traced here: 160 us
  waiting for transfers between devices  85.6 us (53%)
  starting transfers between devices  61.6 us (38%)
  Pallas kernels  8.63 us (5%)
  local copies, waits for them, and re-layouts  3.87 us (2%)
    ppermute x7, waiting for transfers between devices, shifted(): return lax.ppermute(value, AXES, pairs)  69.6 us
    ppermute x7, starting transfers between devices, shifted(): return lax.ppermute(value, AXES, pairs)  37 us
    all_to_all x4, starting transfers between devices, same_half(): lax.all_to_all(value, 'seq', 0, 0, axis_index_groups=groups, tiled=True)  24.6 us
    all_to_all x4, waiting for transfers between devices, same_half(): lax.all_to_all(value, 'seq', 0, 0, axis_index_groups=groups, tiled=True)  16 us
    unnamed x24, local copies, waits for them, and re-layouts  3.83 us
  transfers between devices with their start and end apart: 11, of which 6 were waited for; matrix products, arithmetic and copies ran while one was open for 0% of the time, Pallas kernels for 4%

profile of v3, /device:TPU:1, one launch (start us, length us, event | category | flops | bytes accessed | tf_op | source)
XLA Modules:
  0.0 159.9 jit_solution(693628199570829880)
XLA Ops:
  0.0 0.0 copy-start
  0.0 0.9 copy-done
  1.0 0.0 copy-start.2
  1.0 0.9 copy-done.2
  1.9 0.0 copy-start.4
  1.9 0.9 copy-done.4
  2.9 0.0 copy-start.6
  2.9 0.9 copy-done.6
  3.8 0.0 copy-start.8
  3.8 0.0 copy-start.10
  3.8 0.9 shard_map.83
  4.7 7.7 %all-to-all-start = ((bf16[16,16,1024]{2,1,0:T(8,128)(2,1)}), bf16[16,16,1024]{2,1,0:T(8,128)(2,1)S(1)}, u32[]{:S(2)}, u32[]{:S(2)}) async-start(bf16[16,16,1024]{2,1,0:T(8,128)(2,1)} %shard_map.83), calls=%async_computation | async-start | bytes 1048576 | tf_op jit(solution)/shard_map/all_to_all | solution.py:36
  12.4 0.0 copy-done.8
  12.4 0.0 copy-done.9
  12.5 0.0 copy-done.10
  12.5 0.0 copy-done.11
  12.5 1.8 %shard_map.82.refs_0_ = bf16[256,1536]{1,0:T(8,128)(2,1)S(1)} custom-call(bf16[256,512]{1,0:T(8,128)(2,1)S(1)} %bitcast.20, bf16[256,512]{1,0:T(8,128)(2,1)S(1)} %bitcast.21, bf16[256,512]{1,0:T(8,128)(2,1)S(1)} %bitcast.22, bf16[256,512]{1,0:T(8,128)(2,1)S(1)} %bitcast.23), custom_call_target="tpu_custom_call" | custom-call | flops 335544320 | bytes 1835008 | tf_op jit(solution)/shard_map/pallas_call | solution.py:83
  14.3 0.0 copy-done.1
  14.3 0.0 copy-done.3
  14.3 0.0 copy-done.5
  14.4 0.0 copy-done.7
  14.4 0.9 shard_map.84
  15.3 6.2 %all-to-all-done.own_ref = bf16[16,16,1024]{2,1,0:T(8,128)(2,1)S(1)} async-done(((bf16[16,16,1024]{2,1,0:T(8,128)(2,1)}), bf16[16,16,1024]{2,1,0:T(8,128)(2,1)S(1)}, u32[]{:S(2)}, u32[]{:S(2)}) %all-to-all-start) | async-done | bytes 524320 | tf_op jit(solution)/shard_map/all_to_all | solution.py:36
  21.4 3.6 %all-to-all-start.1 = ((bf16[16,16,1024]{2,1,0:T(8,128)(2,1)}), bf16[16,16,1024]{2,1,0:T(8,128)(2,1)S(1)}, u32[]{:S(2)}, u32[]{:S(2)}) async-start(bf16[16,16,1024]{2,1,0:T(8,128)(2,1)} %shard_map.84), calls=%async_computation.1 | async-start | bytes 1048576 | tf_op jit(solution)/shard_map/all_to_all | solution.py:36
  25.0 16.9 %collective-permute-start.1 = (bf16[16,8,1024]{2,1,0:T(8,128)(2,1)S(1)}, bf16[16,8,1024]{2,1,0:T(8,128)(2,1)S(1)}, u32[]{:S(2)}, u32[]{:S(2)}) collective-permute-start(bf16[16,8,1024]{2,1,0:T(8,128)(2,1)S(1)} %slice.8), channel_id=1, source_target_pairs={{32,33},{33,32},{34,35},{35,34},{36,37},{37,36},{38,39},{39,38},{4... | collective-permute-start | bytes 786440 | tf_op jit(solution)/shard_map/ppermute | solution.py:30
  42.0 0.0 all-to-all-done.1.own_ref
  42.0 9.6 %collective-permute-start.4 = (bf16[16,8,1024]{2,1,0:T(8,128)(2,1)S(1)}, bf16[16,8,1024]{2,1,0:T(8,128)(2,1)S(1)}, u32[]{:S(2)}, u32[]{:S(2)}) collective-permute-start(bf16[16,8,1024]{2,1,0:T(8,128)(2,1)S(1)} %slice.9.refs_0_), channel_id=1, source_target_pairs={{32,33},{33,32},{34,35},{35,34},{36,37},{37,36},{38,39},{39,38},{4... | collective-permute-start | bytes 786440 | tf_op jit(solution)/shard_map/ppermute | solution.py:30
  51.7 0.0 collective-permute-done.1.far_ref
  51.7 1.1 shard_map.85
  52.8 1.9 %collective-permute-start.2 = (bf16[16,8,768]{2,1,0:T(8,128)(2,1)S(1)}, bf16[16,8,768]{2,1,0:T(8,128)(2,1)S(1)}, u32[]{:S(2)}, u32[]{:S(2)}) collective-permute-start(bf16[16,8,768]{2,1,0:T(8,128)(2,1)S(1)} %get-tuple-element.9), channel_id=1, source_target_pairs={{32,0},{33,1},{34,2},{35,3},{36,4},{37,5},{38,6},{39,7},{40,8},{41... | collective-permute-start | bytes 589832 | tf_op jit(solution)/shard_map/ppermute | solution.py:30
  54.7 2.8 %collective-permute-start.3 = (bf16[16,8,768]{2,1,0:T(8,128)(2,1)S(1)}, bf16[16,8,768]{2,1,0:T(8,128)(2,1)S(1)}, u32[]{:S(2)}, u32[]{:S(2)}) collective-permute-start(bf16[16,8,768]{2,1,0:T(8,128)(2,1)S(1)} %get-tuple-element.10), channel_id=1, source_target_pairs={{32,1},{33,0},{34,3},{35,2},{36,5},{37,4},{38,7},{39,6},{40,9},{41... | collective-permute-start | bytes 589832 | tf_op jit(solution)/shard_map/ppermute | solution.py:30
  57.5 1.9 %collective-permute-start = (bf16[256,1536]{1,0:T(8,128)(2,1)S(1)}, bf16[256,1536]{1,0:T(8,128)(2,1)S(1)}, u32[]{:S(2)}, u32[]{:S(2)}) collective-permute-start(bf16[256,1536]{1,0:T(8,128)(2,1)S(1)} %shard_map.82.refs_0_), channel_id=1, source_target_pairs={{32,0},{33,1},{34,2},{35,3},{36,4},{37,5},{38,6},{39,7},{40,8},{41... | collective-permute-start | bytes 2359304 | tf_op jit(solution)/shard_map/ppermute | solution.py:30
  59.4 17.1 %collective-permute-done.4.far_ref = bf16[16,8,1024]{2,1,0:T(8,128)(2,1)S(1)} collective-permute-done((bf16[16,8,1024]{2,1,0:T(8,128)(2,1)S(1)}, bf16[16,8,1024]{2,1,0:T(8,128)(2,1)S(1)}, u32[]{:S(2)}, u32[]{:S(2)}) %collective-permute-start.4) | collective-permute-done | bytes 262176 | tf_op jit(solution)/shard_map/ppermute | solution.py:30
  76.5 1.1 shard_map.86
  77.6 17.5 %collective-permute-done.2.own_ref = bf16[16,8,768]{2,1,0:T(8,128)(2,1)S(1)} collective-permute-done((bf16[16,8,768]{2,1,0:T(8,128)(2,1)S(1)}, bf16[16,8,768]{2,1,0:T(8,128)(2,1)S(1)}, u32[]{:S(2)}, u32[]{:S(2)}) %collective-permute-start.2) | collective-permute-done | bytes 196640 | tf_op jit(solution)/shard_map/ppermute | solution.py:30
  95.0 16.6 %collective-permute-done.3.far_ref = bf16[16,8,768]{2,1,0:T(8,128)(2,1)S(1)} collective-permute-done((bf16[16,8,768]{2,1,0:T(8,128)(2,1)S(1)}, bf16[16,8,768]{2,1,0:T(8,128)(2,1)S(1)}, u32[]{:S(2)}, u32[]{:S(2)}) %collective-permute-start.3) | collective-permute-done | bytes 196640 | tf_op jit(solution)/shard_map/ppermute | solution.py:30
  111.6 0.8 shard_map.87
  112.4 6.6 %all-to-all-start.2 = ((bf16[16,16,768]{2,1,0:T(8,128)(2,1)}), bf16[16,16,768]{2,1,0:T(8,128)(2,1)S(1)}, u32[]{:S(2)}, u32[]{:S(2)}) async-start(bf16[16,16,768]{2,1,0:T(8,128)(2,1)} %shard_map.87), calls=%async_computation.2 | async-start | bytes 786432 | tf_op jit(solution)/shard_map/all_to_all | solution.py:36
  119.0 1.9 %collective-permute-start.6 = (bf16[16,8,768]{2,1,0:T(8,128)(2,1)S(1)}, bf16[16,8,768]{2,1,0:T(8,128)(2,1)S(1)}, u32[]{:S(2)}, u32[]{:S(2)}) collective-permute-start(bf16[16,8,768]{2,1,0:T(8,128)(2,1)S(1)} %get-tuple-element.12), channel_id=1, source_target_pairs={{32,1},{33,0},{34,3},{35,2},{36,5},{37,4},{38,7},{39,6},{40,9},{41... | collective-permute-start | bytes 589832 | tf_op jit(solution)/shard_map/ppermute | solution.py:30
  120.9 1.9 %collective-permute-start.5 = (bf16[16,8,768]{2,1,0:T(8,128)(2,1)S(1)}, bf16[16,8,768]{2,1,0:T(8,128)(2,1)S(1)}, u32[]{:S(2)}, u32[]{:S(2)}) collective-permute-start(bf16[16,8,768]{2,1,0:T(8,128)(2,1)S(1)} %get-tuple-element.11.refs_0_), channel_id=1, source_target_pairs={{32,0},{33,1},{34,2},{35,3},{36,4},{37,5},{38,6},{39,7},{40,8},{41... | collective-permute-start | bytes 589832 | tf_op jit(solution)/shard_map/ppermute | solution.py:30
  122.9 18.4 %collective-permute-done.6.far_ref = bf16[16,8,768]{2,1,0:T(8,128)(2,1)S(1)} collective-permute-done((bf16[16,8,768]{2,1,0:T(8,128)(2,1)S(1)}, bf16[16,8,768]{2,1,0:T(8,128)(2,1)S(1)}, u32[]{:S(2)}, u32[]{:S(2)}) %collective-permute-start.6) | collective-permute-done | bytes 196640 | tf_op jit(solution)/shard_map/ppermute | solution.py:30
  141.3 0.0 collective-permute-done.5.own_ref
  141.3 0.8 shard_map.88
  142.1 0.0 all-to-all-done.2.refs_0_
  142.1 6.7 %all-to-all-start.3 = ((bf16[16,16,768]{2,1,0:T(8,128)(2,1)}), bf16[16,16,768]{2,1,0:T(8,128)(2,1)S(1)}, u32[]{:S(2)}, u32[]{:S(2)}) async-start(bf16[16,16,768]{2,1,0:T(8,128)(2,1)} %shard_map.88), calls=%async_computation.3 | async-start | bytes 786432 | tf_op jit(solution)/shard_map/all_to_all | solution.py:36
  148.7 0.0 collective-permute-done
  148.7 9.8 %all-to-all-done.3.refs_1_ = bf16[16,16,768]{2,1,0:T(8,128)(2,1)S(1)} async-done(((bf16[16,16,768]{2,1,0:T(8,128)(2,1)}), bf16[16,16,768]{2,1,0:T(8,128)(2,1)S(1)}, u32[]{:S(2)}, u32[]{:S(2)}) %all-to-all-start.3) | async-done | bytes 393248 | tf_op jit(solution)/shard_map/all_to_all | solution.py:36
  158.6 1.3 shard_map.89
  (8 shorter events, 0.0 us)
Async XLA Ops:
  0.0 0.9 copy-start
  1.0 0.9 copy-start.2
  1.9 0.9 copy-start.4
  2.9 0.9 copy-start.6
  3.8 8.6 %copy-start.8 = (bf16[1,256,512]{2,1,0:T(8,128)(2,1)S(1)}, bf16[1,256,512]{2,1,0:T(8,128)(2,1)}, u32[]{:S(2)}) copy-start(bf16[1,256,512]{2,1,0:T(8,128)(2,1)} %param.8) | copy-start | bytes 786436
  3.8 8.6 %copy-start.9 = (bf16[1,256,512]{2,1,0:T(8,128)(2,1)S(1)}, bf16[1,256,512]{2,1,0:T(8,128)(2,1)}, u32[]{:S(2)}) copy-start(bf16[1,256,512]{2,1,0:T(8,128)(2,1)} %param.9) | copy-start | bytes 786436
  3.8 8.6 %copy-start.10 = (bf16[1,256,512]{2,1,0:T(8,128)(2,1)S(1)}, bf16[1,256,512]{2,1,0:T(8,128)(2,1)}, u32[]{:S(2)}) copy-start(bf16[1,256,512]{2,1,0:T(8,128)(2,1)} %param.10) | copy-start | bytes 786436
  3.8 8.7 %copy-start.11 = (bf16[1,256,512]{2,1,0:T(8,128)(2,1)S(1)}, bf16[1,256,512]{2,1,0:T(8,128)(2,1)}, u32[]{:S(2)}) copy-start(bf16[1,256,512]{2,1,0:T(8,128)(2,1)} %param.11) | copy-start | bytes 786436
  4.7 9.6 %copy-start.1 = (bf16[1,256,512]{2,1,0:T(8,128)(2,1)S(1)}, bf16[1,256,512]{2,1,0:T(8,128)(2,1)}, u32[]{:S(2)}) copy-start(bf16[1,256,512]{2,1,0:T(8,128)(2,1)} %param.12) | copy-start | bytes 786436
  4.7 9.6 %copy-start.3 = (bf16[1,256,512]{2,1,0:T(8,128)(2,1)S(1)}, bf16[1,256,512]{2,1,0:T(8,128)(2,1)}, u32[]{:S(2)}) copy-start(bf16[1,256,512]{2,1,0:T(8,128)(2,1)} %param.13) | copy-start | bytes 786436
  4.7 9.7 %copy-start.5 = (bf16[1,256,512]{2,1,0:T(8,128)(2,1)S(1)}, bf16[1,256,512]{2,1,0:T(8,128)(2,1)}, u32[]{:S(2)}) copy-start(bf16[1,256,512]{2,1,0:T(8,128)(2,1)} %param.14) | copy-start | bytes 786436
  4.7 9.7 %copy-start.7 = (bf16[1,256,512]{2,1,0:T(8,128)(2,1)S(1)}, bf16[1,256,512]{2,1,0:T(8,128)(2,1)}, u32[]{:S(2)}) copy-start(bf16[1,256,512]{2,1,0:T(8,128)(2,1)} %param.15) | copy-start | bytes 786436
  4.7 16.7 %all-to-all-start = ((bf16[16,16,1024]{2,1,0:T(8,128)(2,1)}), bf16[16,16,1024]{2,1,0:T(8,128)(2,1)S(1)}, u32[]{:S(2)}, u32[]{:S(2)}) async-start(bf16[16,16,1024]{2,1,0:T(8,128)(2,1)} %shard_map.83), calls=%async_computation | async-start | bytes 1048576 | tf_op jit(solution)/shard_map/all_to_all | solution.py:36
  21.4 20.6 %all-to-all-start.1 = ((bf16[16,16,1024]{2,1,0:T(8,128)(2,1)}), bf16[16,16,1024]{2,1,0:T(8,128)(2,1)S(1)}, u32[]{:S(2)}, u32[]{:S(2)}) async-start(bf16[16,16,1024]{2,1,0:T(8,128)(2,1)} %shard_map.84), calls=%async_computation.1 | async-start | bytes 1048576 | tf_op jit(solution)/shard_map/all_to_all | solution.py:36
  25.0 26.6 %collective-permute-start.1 = (bf16[16,8,1024]{2,1,0:T(8,128)(2,1)S(1)}, bf16[16,8,1024]{2,1,0:T(8,128)(2,1)S(1)}, u32[]{:S(2)}, u32[]{:S(2)}) collective-permute-start(bf16[16,8,1024]{2,1,0:T(8,128)(2,1)S(1)} %slice.8), channel_id=1, source_target_pairs={{32,33},{33,32},{34,35},{35,34},{36,37},{37,36},{38,39},{39,38},{4... | collective-permute-start | bytes 786440 | tf_op jit(solution)/shard_map/ppermute | solution.py:30
  42.0 34.4 %collective-permute-start.4 = (bf16[16,8,1024]{2,1,0:T(8,128)(2,1)S(1)}, bf16[16,8,1024]{2,1,0:T(8,128)(2,1)S(1)}, u32[]{:S(2)}, u32[]{:S(2)}) collective-permute-start(bf16[16,8,1024]{2,1,0:T(8,128)(2,1)S(1)} %slice.9.refs_0_), channel_id=1, source_target_pairs={{32,33},{33,32},{34,35},{35,34},{36,37},{37,36},{38,39},{39,38},{4... | collective-permute-start | bytes 786440 | tf_op jit(solution)/shard_map/ppermute | solution.py:30
  52.8 42.3 %collective-permute-start.2 = (bf16[16,8,768]{2,1,0:T(8,128)(2,1)S(1)}, bf16[16,8,768]{2,1,0:T(8,128)(2,1)S(1)}, u32[]{:S(2)}, u32[]{:S(2)}) collective-permute-start(bf16[16,8,768]{2,1,0:T(8,128)(2,1)S(1)} %get-tuple-element.9), channel_id=1, source_target_pairs={{32,0},{33,1},{34,2},{35,3},{36,4},{37,5},{38,6},{39,7},{40,8},{41... | collective-permute-start | bytes 589832 | tf_op jit(solution)/shard_map/ppermute | solution.py:30
  54.7 57.0 %collective-permute-start.3 = (bf16[16,8,768]{2,1,0:T(8,128)(2,1)S(1)}, bf16[16,8,768]{2,1,0:T(8,128)(2,1)S(1)}, u32[]{:S(2)}, u32[]{:S(2)}) collective-permute-start(bf16[16,8,768]{2,1,0:T(8,128)(2,1)S(1)} %get-tuple-element.10), channel_id=1, source_target_pairs={{32,1},{33,0},{34,3},{35,2},{36,5},{37,4},{38,7},{39,6},{40,9},{41... | collective-permute-start | bytes 589832 | tf_op jit(solution)/shard_map/ppermute | solution.py:30
  57.5 91.3 %collective-permute-start = (bf16[256,1536]{1,0:T(8,128)(2,1)S(1)}, bf16[256,1536]{1,0:T(8,128)(2,1)S(1)}, u32[]{:S(2)}, u32[]{:S(2)}) collective-permute-start(bf16[256,1536]{1,0:T(8,128)(2,1)S(1)} %shard_map.82.refs_0_), channel_id=1, source_target_pairs={{32,0},{33,1},{34,2},{35,3},{36,4},{37,5},{38,6},{39,7},{40,8},{41... | collective-permute-start | bytes 2359304 | tf_op jit(solution)/shard_map/ppermute | solution.py:30
  112.4 29.6 %all-to-all-start.2 = ((bf16[16,16,768]{2,1,0:T(8,128)(2,1)}), bf16[16,16,768]{2,1,0:T(8,128)(2,1)S(1)}, u32[]{:S(2)}, u32[]{:S(2)}) async-start(bf16[16,16,768]{2,1,0:T(8,128)(2,1)} %shard_map.87), calls=%async_computation.2 | async-start | bytes 786432 | tf_op jit(solution)/shard_map/all_to_all | solution.py:36
  119.0 22.3 %collective-permute-start.6 = (bf16[16,8,768]{2,1,0:T(8,128)(2,1)S(1)}, bf16[16,8,768]{2,1,0:T(8,128)(2,1)S(1)}, u32[]{:S(2)}, u32[]{:S(2)}) collective-permute-start(bf16[16,8,768]{2,1,0:T(8,128)(2,1)S(1)} %get-tuple-element.12), channel_id=1, source_target_pairs={{32,1},{33,0},{34,3},{35,2},{36,5},{37,4},{38,7},{39,6},{40,9},{41... | collective-permute-start | bytes 589832 | tf_op jit(solution)/shard_map/ppermute | solution.py:30
  120.9 20.3 %collective-permute-start.5 = (bf16[16,8,768]{2,1,0:T(8,128)(2,1)S(1)}, bf16[16,8,768]{2,1,0:T(8,128)(2,1)S(1)}, u32[]{:S(2)}, u32[]{:S(2)}) collective-permute-start(bf16[16,8,768]{2,1,0:T(8,128)(2,1)S(1)} %get-tuple-element.11.refs_0_), channel_id=1, source_target_pairs={{32,0},{33,1},{34,2},{35,3},{36,4},{37,5},{38,6},{39,7},{40,8},{41... | collective-permute-start | bytes 589832 | tf_op jit(solution)/shard_map/ppermute | solution.py:30
  142.1 16.5 %all-to-all-start.3 = ((bf16[16,16,768]{2,1,0:T(8,128)(2,1)}), bf16[16,16,768]{2,1,0:T(8,128)(2,1)S(1)}, u32[]{:S(2)}, u32[]{:S(2)}) async-start(bf16[16,16,768]{2,1,0:T(8,128)(2,1)} %shard_map.88), calls=%async_computation.3 | async-start | bytes 786432 | tf_op jit(solution)/shard_map/all_to_all | solution.py:36

commit v4 on v2

v4 whole, which is shorter than its diff:
```python
import functools

import jax
import jax.numpy as jnp
from jax import lax
from jax.experimental import pallas as pl
from jax.experimental.pallas import tpu as pltpu
from jax.sharding import PartitionSpec as P

H_ROW = 4
H_COL = 4
HD = 128
COLS = 256
LOG2E = 1.4426950408889634
VMEM = pl.BlockSpec(memory_space=pltpu.VMEM)
LEFT = pl.BlockSpec(memory_space=pl.ANY)
PARAMS = pltpu.CompilerParams(vmem_limit_bytes=24 * 1024 * 1024)


def from_behind(value, axis, steps):
    count = lax.axis_size(axis)
    leading, last = (max(0, -steps), min(count, count - steps))
    return lax.ppermute(value, axis, [(source, source + steps) for source in range(leading, last)])


def dot(a, b, over_a, over_b):
    dims = (((over_a,), (over_b,)), ((), ()))
    return lax.dot_general(a, b, dims, preferred_element_type=jnp.float32)


def head_back(queries, keys, values, grad_out, allowed):
    scaling = HD ** (-0.5)
    scores = jnp.where(allowed, dot(keys, queries, 1, 1), -1e30)
    largest = jnp.max(scores, axis=0, keepdims=True)
    weights = jnp.exp2((scores - largest) * (scaling * LOG2E))
    probability = weights * (1.0 / jnp.sum(weights, axis=0, keepdims=True))
    prob_low = probability.astype(jnp.bfloat16)
    grad_probs = dot(values, grad_out, 1, 1)
    inner_sum = jnp.sum(prob_low.astype(jnp.float32) * grad_probs, axis=0, keepdims=True)
    grad_low = (probability * ((grad_probs - inner_sum) * scaling)).astype(jnp.bfloat16)
    return (
        dot(grad_low, keys, 0, 0).astype(jnp.bfloat16),
        dot(grad_low, queries, 1, 0).astype(jnp.bfloat16),
        dot(prob_low, grad_out, 1, 0).astype(jnp.bfloat16),
    )


def cost(heads, tokens):
    pairs = heads * tokens * tokens
    return pl.CostEstimate(
        flops=10 * pairs * HD, bytes_accessed=14 * tokens * heads * HD, transcendentals=pairs
    )


def moved(nbytes):
    return pl.CostEstimate(flops=0, bytes_accessed=2 * nbytes, transcendentals=0)


def row_kernel(q_hbm, k_hbm, v_hbm, g_hbm, out_ref, held, sems):
    tokens = out_ref.shape[0]
    copies = [
        pltpu.make_async_copy(ref, held.at[i], sems.at[i])
        for i, ref in enumerate((q_hbm, k_hbm, v_hbm, g_hbm))
    ]
    for copy in copies:
        copy.start()
    key_at = lax.broadcasted_iota(jnp.int32, (tokens, tokens), 0)
    query_at = lax.broadcasted_iota(jnp.int32, (tokens, tokens), 1)
    allowed = query_at >= key_at
    for copy in copies:
        copy.wait()
    for h in range(H_ROW):
        taken = [held[i, :, h * HD : (h + 1) * HD] for i in range(4)]
        for i, grad in enumerate(head_back(*taken, allowed)):
            at = i * H_ROW + h
            out_ref[:, at * HD : (at + 1) * HD] = grad


def row_grads(*operands):
    tokens, width = operands[0].shape
    return pl.pallas_call(
        row_kernel,
        in_specs=[LEFT] * 4,
        out_specs=VMEM,
        out_shape=jax.ShapeDtypeStruct((tokens, 3 * width), jnp.bfloat16),
        scratch_shapes=[
            pltpu.VMEM((4, tokens, width), jnp.bfloat16),
            pltpu.SemaphoreType.DMA((4,)),
        ],
        compiler_params=PARAMS,
        cost_estimate=cost(H_ROW, tokens),
    )(*operands)


def col_kernel(group, in_ref, out_ref):
    tokens = out_ref.shape[0]
    key_at = lax.broadcasted_iota(jnp.int32, (tokens, tokens), 0)
    query_at = lax.broadcasted_iota(jnp.int32, (tokens, tokens), 1)
    same = lax.rem(query_at, group) == lax.rem(key_at, group)
    allowed = (query_at >= key_at) & same
    for h in range(H_COL):
        lanes = [slice((i * H_COL + h) * HD, (i * H_COL + h + 1) * HD) for i in range(4)]
        taken = [in_ref[:, lane] for lane in lanes]
        for lane, grad in zip(lanes, head_back(*taken, allowed)):
            out_ref[:, lane] = grad


def col_grads(group, operand):
    tokens, lanes = operand.shape
    return pl.pallas_call(
        functools.partial(col_kernel, group),
        in_specs=[VMEM],
        out_specs=VMEM,
        out_shape=jax.ShapeDtypeStruct((tokens, 3 * lanes // 4), jnp.bfloat16),
        compiler_params=PARAMS,
        cost_estimate=cost(H_COL, tokens),
    )(operand)


def keep_kernel(in_ref, after_ref, out_ref):
    out_ref[...] = in_ref[...]


def keep(value, after):
    return pl.pallas_call(
        keep_kernel,
        in_specs=[VMEM, LEFT],
        out_specs=VMEM,
        out_shape=jax.ShapeDtypeStruct(value.shape, value.dtype),
        compiler_params=PARAMS,
        cost_estimate=moved(2 * value.size),
    )(value, after)


def place_kernel(row_ref, col_ref, out_ref):
    width = row_ref.shape[1] // 3
    for i in range(3):
        lanes = slice(i * width, (i + 1) * width)
        out_ref[:, 2 * i * width : (2 * i + 1) * width] = row_ref[:, lanes]
        out_ref[:, (2 * i + 1) * width : (2 * i + 2) * width] = col_ref[:, lanes]


def place(row_part, col_part):
    tokens, lanes = row_part.shape
    return pl.pallas_call(
        place_kernel,
        in_specs=[VMEM] * 2,
        out_specs=VMEM,
        out_shape=jax.ShapeDtypeStruct((tokens, 2 * lanes), jnp.bfloat16),
        compiler_params=PARAMS,
        cost_estimate=moved(4 * tokens * lanes),
    )(row_part, col_part)


def exchanged(value):
    return lax.all_to_all(value, "seq", split_axis=0, concat_axis=0, tiled=True)


def col_path(query_col, key_col, value_col, cotangent_col):
    tokens_dev, width = query_col.shape
    groups = lax.axis_size("seq")
    group = COLS // groups
    sent = jnp.concatenate([query_col, key_col, value_col, cotangent_col], axis=-1)
    arrived = exchanged(sent.reshape(groups, group, 4 * width))
    grads = col_grads(group, arrived.reshape(groups * group, 4 * width))
    back = exchanged(grads.reshape(groups, group, 3 * width))
    return back.reshape(tokens_dev, 3 * width)


def no_col_path(query_col, key_col, value_col, cotangent_col):
    tokens_dev, width = query_col.shape
    return jnp.zeros((tokens_dev, 3 * width), query_col.dtype)


def on_device(
    query_row, key_row, value_row, cotangent_row, query_col, key_col, value_col, cotangent_col
):
    row_part = row_grads(query_row[0], key_row[0], value_row[0], cotangent_row[0])
    row_pack = from_behind(row_part, "section", -1)
    col_part = lax.cond(
        lax.axis_index("section") > 0,
        col_path,
        no_col_path,
        query_col[0],
        key_col[0],
        value_col[0],
        cotangent_col[0],
    )
    col_pack = from_behind(keep(col_part, row_pack), "section", -1)
    return place(row_pack, col_pack)[None]


def solution(mesh):
    return jax.shard_map(
        on_device,
        mesh=mesh,
        in_specs=(P("section", "seq", None),) * 8,
        out_specs=P("section", "seq", None),
        check_vma=False,
    )
```

time: 160 us -> 139 us (0.87)
  waiting for transfers between devices: 78.6 us -> 50.2 us
  blocking collectives: 48 us -> 68.2 us
  starting transfers between devices: 26 us -> 10.7 us
  local copies, waits for them, and re-layouts: 1.3 us -> 3.81 us
  other arithmetic: 2.28 us -> 0.11 us
    ppermute x2, waiting for transfers between devices: 78.6 us -> 50.2 us  [from_behind(): lax.ppermute(value, axis, [(source, source + steps) for source in range(l...]
    all_to_all x1 -> x0, starting transfers between devices: 21.3 us -> none  [on_device(): lax.all_to_all(sent, 'seq', split_axis=0, concat_axis=0, tiled=True)]
    all_to_all x1 -> x2, blocking collectives: 48 us -> 68.2 us  [exchanged(): return lax.all_to_all(value, 'seq', split_axis=0, concat_axis=0, tiled=True)]
    ppermute x2, starting transfers between devices: 4.77 us -> 10.7 us  [from_behind(): lax.ppermute(value, axis, [(source, source + steps) for source in range(l...]
    unnamed x15 -> x16, local copies, waits for them, and re-layouts: 1.28 us -> 3.81 us
    concatenate x1, other arithmetic: 2.28 us -> 0.11 us  [col_path(): jnp.concatenate([query_col, key_col, value_col, cotangent_col], axis=-1)]
    pallas_call x2 -> x4, Pallas kernels: 3.7 us -> 5.14 us  [the longest x1 1.98 us: row_grads(): pl.pallas_call(row_kernel, in_specs=[LEFT] * 4, out_specs=VMEM, out_shape...]
  transfers between devices with their start and end apart: 3 -> 2, of which waited for: 2 -> 1; matrix products, arithmetic and copies ran while one was open for 0% -> 0% of each run, Pallas kernels for 1% -> 1%
where the time goes in v4:
time: 139 us; the launch traced here: 138 us
  blocking collectives  68.2 us (49%)
  waiting for transfers between devices  50.2 us (36%)
  starting transfers between devices  10.7 us (8%)
  Pallas kernels  5.14 us (4%)
  local copies, waits for them, and re-layouts  3.81 us (3%)
    all_to_all x2, blocking collectives, exchanged(): return lax.all_to_all(value, 'seq', split_axis=0, concat_axis=0, tiled=True)  68.2 us
    ppermute x2, waiting for transfers between devices, from_behind(): lax.ppermute(value, axis, [(source, source + steps) for source in range(l...  50.2 us
    ppermute x2, starting transfers between devices, from_behind(): lax.ppermute(value, axis, [(source, source + steps) for source in range(l...  10.7 us
    unnamed x16, local copies, waits for them, and re-layouts  3.81 us
  transfers between devices with their start and end apart: 2, of which 1 were waited for; matrix products, arithmetic and copies ran while one was open for 0% of the time, Pallas kernels for 1%

profile of v4, /device:TPU:1, one launch (start us, length us, event | category | flops | bytes accessed | tf_op | source)
XLA Modules:
  0.0 138.4 jit_solution(7950595733502469953)
XLA Ops:
  0.0 0.0 copy-start
  0.0 0.9 copy-done
  1.0 0.0 copy-start.1
  1.0 0.9 copy-done.1
  1.9 0.0 copy-start.2
  1.9 0.9 copy-done.2
  2.9 0.0 copy-start.3
  2.9 0.9 copy-done.3
  3.8 0.0 copy-start.4
  3.8 0.0 copy-start.5
  3.8 0.0 copy-start.6
  3.8 0.0 copy-start.7
  3.8 2.0 %shard_map.86 = bf16[256,1536]{1,0:T(8,128)(2,1)S(1)} custom-call(bf16[256,512]{1,0:T(8,128)(2,1)S(1)} %bitcast.14, bf16[256,512]{1,0:T(8,128)(2,1)S(1)} %bitcast.15, bf16[256,512]{1,0:T(8,128)(2,1)S(1)} %bitcast.16, bf16[256,512]{1,0:T(8,128)(2,1)S(1)} %bitcast.17), custom_call_target="tpu_custom_call" | custom-call | flops 335544320 | bytes 1835008 | tf_op jit(solution)/shard_map/pallas_call | solution.py:81
  5.8 8.8 %collective-permute-start = (bf16[256,1536]{1,0:T(8,128)(2,1)S(1)}, bf16[256,1536]{1,0:T(8,128)(2,1)S(1)}, u32[]{:S(2)}, u32[]{:S(2)}) collective-permute-start(bf16[256,1536]{1,0:T(8,128)(2,1)S(1)} %shard_map.86), channel_id=1, source_target_pairs={{32,0},{64,32},{96,64},{128,96},{160,128},{192,160},{224,192},{256... | collective-permute-start | bytes 2359304 | tf_op jit(solution)/shard_map/ppermute | solution.py:23
  14.6 0.0 copy-done.4
  14.6 0.0 copy-done.5
  14.6 0.0 copy-done.6
  14.6 0.0 copy-done.7
  14.6 70.2 %conditional.1 = (bf16[256,1536]{1,0:T(8,128)(2,1)S(1)}) conditional(s32[]{:T(128)} %convert_element_type.3, () %tuple.11, (bf16[1,256,512]{2,1,0:T(8,128)(2,1)S(1)}, bf16[1,256,512]{2,1,0:T(8,128)(2,1)S(1)}, bf16[1,256,512]{2,1,0:T(8,128)(2,1)S(1)}, bf16[1,256,512]{2,1,0:T(8,128)(2,1)S(1)}) %tuple.18), branch_computations={%region_0.0_spmd, %region_1.0_spmd} | conditional | flops 339738624 | bytes 7602184 | solution.py:180
  14.7 0.1 pad_maximum_fusion
  14.8 36.4 %all_to_all.8 = bf16[32,8,2048]{2,1,0:T(8,128)(2,1)S(1)} all-to-all(bf16[32,8,2048]{2,1,0:T(8,128)(2,1)S(1)} %pad_maximum_fusion), channel_id=1, replica_groups=mesh['section'=16,'seq'=32] {'seq'}, dimensions={0} | all-to-all | bytes 2097152 | tf_op jit(solution)/shard_map/cond/branch_1_fun/all_to_all | solution.py:156
  51.2 1.8 %branch_1_fun.1 = bf16[256,1536]{1,0:T(8,128)(2,1)S(1)} custom-call(bf16[256,2048]{1,0:T(8,128)(2,1)S(1)} %bitcast.12), custom_call_target="tpu_custom_call" | custom-call | flops 335544320 | bytes 1835008 | tf_op jit(solution)/shard_map/cond/branch_1_fun/pallas_call | solution.py:110
  53.0 31.8 %all_to_all.9 = bf16[32,8,1536]{2,1,0:T(8,128)(2,1)S(1)} all-to-all(bf16[32,8,1536]{2,1,0:T(8,128)(2,1)S(1)} %bitcast.13), channel_id=1, replica_groups=mesh['section'=16,'seq'=32] {'seq'}, dimensions={0} | all-to-all | bytes 1572864 | tf_op jit(solution)/shard_map/cond/branch_1_fun/all_to_all | solution.py:156
  84.9 0.0 collective-permute-done.after_ref.row_ref
  84.9 0.1 shard_map.87
  84.9 1.9 %collective-permute-start.1 = (bf16[256,1536]{1,0:T(8,128)(2,1)S(1)}, bf16[256,1536]{1,0:T(8,128)(2,1)S(1)}, u32[]{:S(2)}, u32[]{:S(2)}) collective-permute-start(bf16[256,1536]{1,0:T(8,128)(2,1)S(1)} %shard_map.87), channel_id=1, source_target_pairs={{32,0},{64,32},{96,64},{128,96},{160,128},{192,160},{224,192},{256... | collective-permute-start | bytes 2359304 | tf_op jit(solution)/shard_map/ppermute | solution.py:23
  86.9 50.2 %collective-permute-done.1.col_ref = bf16[256,1536]{1,0:T(8,128)(2,1)S(1)} collective-permute-done((bf16[256,1536]{1,0:T(8,128)(2,1)S(1)}, bf16[256,1536]{1,0:T(8,128)(2,1)S(1)}, u32[]{:S(2)}, u32[]{:S(2)}) %collective-permute-start.1) | collective-permute-done | bytes 786464 | tf_op jit(solution)/shard_map/ppermute | solution.py:23
  137.1 1.3 shard_map.88
Async XLA Ops:
  0.0 0.9 copy-start
  1.0 0.9 copy-start.1
  1.9 0.9 copy-start.2
  2.9 0.9 copy-start.3
  3.8 10.8 %copy-start.4 = (bf16[1,256,512]{2,1,0:T(8,128)(2,1)S(1)}, bf16[1,256,512]{2,1,0:T(8,128)(2,1)}, u32[]{:S(2)}) copy-start(bf16[1,256,512]{2,1,0:T(8,128)(2,1)} %param.14) | copy-start | bytes 786436
  3.8 10.8 %copy-start.5 = (bf16[1,256,512]{2,1,0:T(8,128)(2,1)S(1)}, bf16[1,256,512]{2,1,0:T(8,128)(2,1)}, u32[]{:S(2)}) copy-start(bf16[1,256,512]{2,1,0:T(8,128)(2,1)} %param.15) | copy-start | bytes 786436
  3.8 10.8 %copy-start.6 = (bf16[1,256,512]{2,1,0:T(8,128)(2,1)S(1)}, bf16[1,256,512]{2,1,0:T(8,128)(2,1)}, u32[]{:S(2)}) copy-start(bf16[1,256,512]{2,1,0:T(8,128)(2,1)} %param.16) | copy-start | bytes 786436
  3.8 10.8 %copy-start.7 = (bf16[1,256,512]{2,1,0:T(8,128)(2,1)S(1)}, bf16[1,256,512]{2,1,0:T(8,128)(2,1)}, u32[]{:S(2)}) copy-start(bf16[1,256,512]{2,1,0:T(8,128)(2,1)} %param.17) | copy-start | bytes 786436
  5.8 79.1 %collective-permute-start = (bf16[256,1536]{1,0:T(8,128)(2,1)S(1)}, bf16[256,1536]{1,0:T(8,128)(2,1)S(1)}, u32[]{:S(2)}, u32[]{:S(2)}) collective-permute-start(bf16[256,1536]{1,0:T(8,128)(2,1)S(1)} %shard_map.86), channel_id=1, source_target_pairs={{32,0},{64,32},{96,64},{128,96},{160,128},{192,160},{224,192},{256... | collective-permute-start | bytes 2359304 | tf_op jit(solution)/shard_map/ppermute | solution.py:23
  84.9 52.2 %collective-permute-start.1 = (bf16[256,1536]{1,0:T(8,128)(2,1)S(1)}, bf16[256,1536]{1,0:T(8,128)(2,1)S(1)}, u32[]{:S(2)}, u32[]{:S(2)}) collective-permute-start(bf16[256,1536]{1,0:T(8,128)(2,1)S(1)} %shard_map.87), channel_id=1, source_target_pairs={{32,0},{64,32},{96,64},{128,96},{160,128},{192,160},{224,192},{256... | collective-permute-start | bytes 2359304 | tf_op jit(solution)/shard_map/ppermute | solution.py:23

commit v5 on v4

--- a/solution.py
+++ b/solution.py
@@ -87,49 +87,39 @@
             pltpu.VMEM((4, tokens, width), jnp.bfloat16),
             pltpu.SemaphoreType.DMA((4,)),
         ],
-        compiler_params=PARAMS,
         cost_estimate=cost(H_ROW, tokens),
     )(*operands)
 
 
-def col_kernel(group, in_ref, out_ref):
+def col_kernel(group, *refs):
+    ins, out_ref = refs[:-1], refs[-1]
     tokens = out_ref.shape[0]
     key_at = lax.broadcasted_iota(jnp.int32, (tokens, tokens), 0)
     query_at = lax.broadcasted_iota(jnp.int32, (tokens, tokens), 1)
     same = lax.rem(query_at, group) == lax.rem(key_at, group)
     allowed = (query_at >= key_at) & same
-    for h in range(H_COL):
-        lanes = [slice((i * H_COL + h) * HD, (i * H_COL + h + 1) * HD) for i in range(4)]
-        taken = [in_ref[:, lane] for lane in lanes]
-        for lane, grad in zip(lanes, head_back(*taken, allowed)):
-            out_ref[:, lane] = grad
-
-
-def col_grads(group, operand):
-    tokens, lanes = operand.shape
+    done = 0
+    for ref in ins:
+        held = ref.shape[1] // (4 * HD)
+        for h in range(held):
+            lanes = [slice((i * held + h) * HD, (i * held + h + 1) * HD) for i in range(4)]
+            taken = [ref[:, lane] for lane in lanes]
+            for i, grad in enumerate(head_back(*taken, allowed)):
+                at = i * H_COL + done + h
+                out_ref[:, at * HD : (at + 1) * HD] = grad
+        done += held
+
+
+def col_grads(group, operands):
+    tokens = operands[0].shape[0]
     return pl.pallas_call(
         functools.partial(col_kernel, group),
-        in_specs=[VMEM],
+        in_specs=[VMEM] * len(operands),
         out_specs=VMEM,
-        out_shape=jax.ShapeDtypeStruct((tokens, 3 * lanes // 4), jnp.bfloat16),
+        out_shape=jax.ShapeDtypeStruct((tokens, 3 * H_COL * HD), jnp.bfloat16),
         compiler_params=PARAMS,
         cost_estimate=cost(H_COL, tokens),
-    )(operand)
-
-
-def keep_kernel(in_ref, after_ref, out_ref):
-    out_ref[...] = in_ref[...]
-
-
-def keep(value, after):
-    return pl.pallas_call(
-        keep_kernel,
-        in_specs=[VMEM, LEFT],
-        out_specs=VMEM,
-        out_shape=jax.ShapeDtypeStruct(value.shape, value.dtype),
-        compiler_params=PARAMS,
-        cost_estimate=moved(2 * value.size),
-    )(value, after)
+    )(*operands)
 
 
 def place_kernel(row_ref, col_ref, out_ref):
@@ -156,38 +146,50 @@
     return lax.all_to_all(value, "seq", split_axis=0, concat_axis=0, tiled=True)
 
 
-def col_path(query_col, key_col, value_col, cotangent_col):
-    tokens_dev, width = query_col.shape
+def col_path(parts, block):
+    tokens_dev, lanes = block.shape
+    width = lanes // 4
     groups = lax.axis_size("seq")
     group = COLS // groups
-    sent = jnp.concatenate([query_col, key_col, value_col, cotangent_col], axis=-1)
-    arrived = exchanged(sent.reshape(groups, group, 4 * width))
-    grads = col_grads(group, arrived.reshape(groups * group, 4 * width))
-    back = exchanged(grads.reshape(groups, group, 3 * width))
+    arrived, done = [], 0
+    for heads in parts:
+        step = heads * HD
+        sent = block
+        if step < width:
+            first = [i * width + done for i in range(4)]
+            sent = jnp.concatenate([block[:, at : at + step] for at in first], axis=-1)
+        sent = exchanged(sent.reshape(groups, group, 4 * step))
+        arrived.append(sent.reshape(groups * group, 4 * step))
+        done += step
+    back = exchanged(col_grads(group, arrived).reshape(groups, group, 3 * width))
     return back.reshape(tokens_dev, 3 * width)
 
 
-def no_col_path(query_col, key_col, value_col, cotangent_col):
-    tokens_dev, width = query_col.shape
-    return jnp.zeros((tokens_dev, 3 * width), query_col.dtype)
+def no_col_path(block):
+    tokens_dev, lanes = block.shape
+    return jnp.zeros((tokens_dev, 3 * lanes // 4), block.dtype)
 
 
 def on_device(
     query_row, key_row, value_row, cotangent_row, query_col, key_col, value_col, cotangent_col
 ):
+    col_in = jnp.concatenate([query_col[0], key_col[0], value_col[0], cotangent_col[0]], axis=-1)
+    col_in = from_behind(col_in, "section", -1)
     row_part = row_grads(query_row[0], key_row[0], value_row[0], cotangent_row[0])
     row_pack = from_behind(row_part, "section", -1)
-    col_part = lax.cond(
-        lax.axis_index("section") > 0,
-        col_path,
-        no_col_path,
-        query_col[0],
-        key_col[0],
-        value_col[0],
-        cotangent_col[0],
-    )
-    col_pack = from_behind(keep(col_part, row_pack), "section", -1)
-    return place(row_pack, col_pack)[None]
+    section = lax.axis_index("section")
+    place_z = section // 2
+    branch = jnp.where(section == lax.axis_size("section") - 1, 0, jnp.where(place_z == 5, 2, 1))
+    col_part = lax.switch(
+        branch,
+        [
+            no_col_path,
+            functools.partial(col_path, (4,)),
+            functools.partial(col_path, (1, 3)),
+        ],
+        col_in,
+    )
+    return place(row_pack, col_part)[None]
 
 
 def solution(mesh):

time: 139 us -> 126 us (0.906)
  the two profiles are of different devices: /device:TPU:1 before, /device:TPU:449 now
where the time goes in v5:
time: 126 us; the launch traced here: 125 us
  blocking collectives  105 us (83%)
  waiting for transfers between devices  7.18 us (6%)
  Pallas kernels  7.05 us (6%)
  starting transfers between devices  4.94 us (4%)
  other arithmetic  1.29 us (1%)
    all_to_all x2, blocking collectives, exchanged(): return lax.all_to_all(value, 'seq', split_axis=0, concat_axis=0, tiled=True)  105 us
    ppermute x2, waiting for transfers between devices, from_behind(): lax.ppermute(value, axis, [(source, source + steps) for source in range(l...  7.18 us
    ppermute x2, starting transfers between devices, from_behind(): lax.ppermute(value, axis, [(source, source + steps) for source in range(l...  4.94 us
    pallas_call x1, Pallas kernels, row_grads(): pl.pallas_call(row_kernel, in_specs=[LEFT] * 4, out_specs=VMEM, out_shape...  3.95 us
  transfers between devices with their start and end apart: 2, of which 1 were waited for; matrix products, arithmetic and copies ran while one was open for 0% of the time, Pallas kernels for 5%

profile of v5, /device:TPU:449, one launch (start us, length us, event | category | flops | bytes accessed | tf_op | source)
XLA Modules:
  0.0 125.3 jit_solution(16856213296273545453)
XLA Ops:
  0.0 1.3 %pad_maximum_fusion = bf16[256,2048]{1,0:T(8,128)(2,1)S(1)} fusion(bf16[256,512]{1,0:T(8,128)(2,1)} %bitcast.33, bf16[256,512]{1,0:T(8,128)(2,1)} %bitcast.34, bf16[256,512]{1,0:T(8,128)(2,1)} %bitcast.35, bf16[256,512]{1,0:T(8,128)(2,1)} %bitcast.36), kind=kLoop, calls=%fused_computation.2 | loop fusion | flops 4194304 | bytes 2097152 | tf_op jit(solution)/shard_map/concatenate | solution.py:176
  1.3 2.6 %collective-permute-start.1 = (bf16[256,2048]{1,0:T(8,128)(2,1)S(1)}, bf16[256,2048]{1,0:T(8,128)(2,1)S(1)}, u32[]{:S(2)}, u32[]{:S(2)}) collective-permute-start(bf16[256,2048]{1,0:T(8,128)(2,1)S(1)} %pad_maximum_fusion), channel_id=1, source_target_pairs={{32,0},{64,32},{96,64},{128,96},{160,128},{192,160},{224,192},{256... | collective-permute-start | bytes 3145736 | tf_op jit(solution)/shard_map/ppermute | solution.py:23
  3.9 4.0 %shard_map.82 = bf16[256,1536]{1,0:T(8,128)(2,1)} custom-call(bf16[256,512]{1,0:T(8,128)(2,1)} %bitcast.29, bf16[256,512]{1,0:T(8,128)(2,1)} %bitcast.30, bf16[256,512]{1,0:T(8,128)(2,1)} %bitcast.31, bf16[256,512]{1,0:T(8,128)(2,1)} %bitcast.32), custom_call_target="tpu_custom_call" | custom-call | flops 335544320 | bytes 1835008 | tf_op jit(solution)/shard_map/pallas_call | solution.py:81
  7.9 2.4 %collective-permute-start = (bf16[256,1536]{1,0:T(8,128)(2,1)}, bf16[256,1536]{1,0:T(8,128)(2,1)S(1)}, u32[]{:S(2)}, u32[]{:S(2)}) collective-permute-start(bf16[256,1536]{1,0:T(8,128)(2,1)} %shard_map.82), channel_id=1, source_target_pairs={{32,0},{64,32},{96,64},{128,96},{160,128},{192,160},{224,192},{256... | collective-permute-start | bytes 2359304 | tf_op jit(solution)/shard_map/ppermute | solution.py:23
  10.2 7.2 %collective-permute-done.1 = bf16[256,2048]{1,0:T(8,128)(2,1)S(1)} collective-permute-done((bf16[256,2048]{1,0:T(8,128)(2,1)S(1)}, bf16[256,2048]{1,0:T(8,128)(2,1)S(1)}, u32[]{:S(2)}, u32[]{:S(2)}) %collective-permute-start.1) | collective-permute-done | bytes 1048608 | tf_op jit(solution)/shard_map/ppermute | solution.py:23
  17.4 106.7 %conditional.1 = (bf16[256,1536]{1,0:T(8,128)(2,1)S(1)}) conditional(s32[]{:T(128)} %clamp.3, () %tuple.14, bf16[256,2048]{1,0:T(8,128)(2,1)S(1)} %collective-permute-done.1, bf16[256,2048]{1,0:T(8,128)(2,1)S(1)} %collective-permute-done.1), branch_computations={%region_0.1_spmd, %region_1.2_spmd, %region_2.3_spmd} | conditional | flops 339738624 | bytes 9961512 | solution.py:183
  17.4 63.3 %all_to_all.20 = bf16[32,8,2048]{2,1,0:T(8,128)(2,1)S(1)} all-to-all(bf16[32,8,2048]{2,1,0:T(8,128)(2,1)S(1)} %bitcast.26), channel_id=1, replica_groups=mesh['section'=16,'seq'=32] {'seq'}, dimensions={0} | all-to-all | bytes 2097152 | tf_op jit(solution)/shard_map/cond/branch_1_fun/all_to_all | solution.py:146
  80.8 1.8 %branch_1_fun.1 = bf16[256,1536]{1,0:T(8,128)(2,1)S(1)} custom-call(bf16[256,2048]{1,0:T(8,128)(2,1)S(1)} %bitcast.21), custom_call_target="tpu_custom_call" | custom-call | flops 335544320 | bytes 1835008 | tf_op jit(solution)/shard_map/cond/branch_1_fun/pallas_call | solution.py:115
  82.6 41.5 %all_to_all.21 = bf16[32,8,1536]{2,1,0:T(8,128)(2,1)S(1)} all-to-all(bf16[32,8,1536]{2,1,0:T(8,128)(2,1)S(1)} %bitcast.24), channel_id=1, replica_groups=mesh['section'=16,'seq'=32] {'seq'}, dimensions={0} | all-to-all | bytes 1572864 | tf_op jit(solution)/shard_map/cond/branch_1_fun/all_to_all | solution.py:146
  124.1 0.0 collective-permute-done.row_ref
  124.1 1.3 %shard_map.83 = bf16[256,3072]{1,0:T(8,128)(2,1)} custom-call(bf16[256,1536]{1,0:T(8,128)(2,1)S(1)} %collective-permute-done.row_ref, bf16[256,1536]{1,0:T(8,128)(2,1)S(1)} %get-tuple-element.19.col_ref), custom_call_target="tpu_custom_call" | custom-call | bytes 3145728 | tf_op jit(solution)/shard_map/pallas_call | solution.py:135
Async XLA Ops:
  1.3 16.1 %collective-permute-start.1 = (bf16[256,2048]{1,0:T(8,128)(2,1)S(1)}, bf16[256,2048]{1,0:T(8,128)(2,1)S(1)}, u32[]{:S(2)}, u32[]{:S(2)}) collective-permute-start(bf16[256,2048]{1,0:T(8,128)(2,1)S(1)} %pad_maximum_fusion), channel_id=1, source_target_pairs={{32,0},{64,32},{96,64},{128,96},{160,128},{192,160},{224,192},{256... | collective-permute-start | bytes 3145736 | tf_op jit(solution)/shard_map/ppermute | solution.py:23
  7.9 116.2 %collective-permute-start = (bf16[256,1536]{1,0:T(8,128)(2,1)}, bf16[256,1536]{1,0:T(8,128)(2,1)S(1)}, u32[]{:S(2)}, u32[]{:S(2)}) collective-permute-start(bf16[256,1536]{1,0:T(8,128)(2,1)} %shard_map.82), channel_id=1, source_target_pairs={{32,0},{64,32},{96,64},{128,96},{160,128},{192,160},{224,192},{256... | collective-permute-start | bytes 2359304 | tf_op jit(solution)/shard_map/ppermute | solution.py:23

commit v6 on v5

--- a/solution.py
+++ b/solution.py
@@ -39,10 +39,22 @@
     inner_sum = jnp.sum(prob_low.astype(jnp.float32) * grad_probs, axis=0, keepdims=True)
     grad_low = (probability * ((grad_probs - inner_sum) * scaling)).astype(jnp.bfloat16)
     return (
-        dot(grad_low, keys, 0, 0).astype(jnp.bfloat16),
-        dot(grad_low, queries, 1, 0).astype(jnp.bfloat16),
-        dot(prob_low, grad_out, 1, 0).astype(jnp.bfloat16),
-    )
+        dot(grad_low, keys, 0, 0),
+        dot(grad_low, queries, 1, 0),
+        dot(prob_low, grad_out, 1, 0),
+    )
+
+
+def causal_back(queries, keys, values, grad_out, allowed):
+    half = queries.shape[0] // 2
+    early, late = slice(0, half), slice(half, 2 * half)
+    first = head_back(
+        queries[early], keys[early], values[early], grad_out[early], allowed[early, early]
+    )
+    second = head_back(queries[late], keys, values, grad_out[late], allowed[:, late])
+    pairs = [(first[0], second[0])]
+    pairs += [(a + b[early], b[late]) for a, b in zip(first[1:], second[1:])]
+    return [jnp.concatenate(pair, axis=0).astype(jnp.bfloat16) for pair in pairs]
 
 
 def cost(heads, tokens):
@@ -71,7 +83,7 @@
         copy.wait()
     for h in range(H_ROW):
         taken = [held[i, :, h * HD : (h + 1) * HD] for i in range(4)]
-        for i, grad in enumerate(head_back(*taken, allowed)):
+        for i, grad in enumerate(causal_back(*taken, allowed)):
             at = i * H_ROW + h
             out_ref[:, at * HD : (at + 1) * HD] = grad
 
@@ -98,16 +110,14 @@
     query_at = lax.broadcasted_iota(jnp.int32, (tokens, tokens), 1)
     same = lax.rem(query_at, group) == lax.rem(key_at, group)
     allowed = (query_at >= key_at) & same
-    done = 0
-    for ref in ins:
-        held = ref.shape[1] // (4 * HD)
-        for h in range(held):
-            lanes = [slice((i * held + h) * HD, (i * held + h + 1) * HD) for i in range(4)]
-            taken = [ref[:, lane] for lane in lanes]
-            for i, grad in enumerate(head_back(*taken, allowed)):
-                at = i * H_COL + done + h
-                out_ref[:, at * HD : (at + 1) * HD] = grad
-        done += held
+    places = [
+        (ref, slice(at, at + HD)) for ref in ins for at in range(0, ref.shape[1], HD)
+    ]
+    for h in range(H_COL):
+        taken = [ref[:, lane] for ref, lane in places[h::H_COL]]
+        for i, grad in enumerate(causal_back(*taken, allowed)):
+            at = i * H_COL + h
+            out_ref[:, at * HD : (at + 1) * HD] = grad
 
 
 def col_grads(group, operands):
@@ -146,23 +156,18 @@
     return lax.all_to_all(value, "seq", split_axis=0, concat_axis=0, tiled=True)
 
 
-def col_path(parts, block):
+def col_path(first, block):
     tokens_dev, lanes = block.shape
-    width = lanes // 4
     groups = lax.axis_size("seq")
     group = COLS // groups
-    arrived, done = [], 0
-    for heads in parts:
-        step = heads * HD
-        sent = block
-        if step < width:
-            first = [i * width + done for i in range(4)]
-            sent = jnp.concatenate([block[:, at : at + step] for at in first], axis=-1)
-        sent = exchanged(sent.reshape(groups, group, 4 * step))
-        arrived.append(sent.reshape(groups * group, 4 * step))
-        done += step
-    back = exchanged(col_grads(group, arrived).reshape(groups, group, 3 * width))
-    return back.reshape(tokens_dev, 3 * width)
+    arrived = []
+    for part in (block[:, :first], block[:, first:]) if first else (block,):
+        width = part.shape[1]
+        sent = exchanged(part.reshape(groups, group, width))
+        arrived.append(sent.reshape(groups * group, width))
+    grads = col_grads(group, arrived)
+    back = exchanged(grads.reshape(groups, group, grads.shape[1]))
+    return back.reshape(tokens_dev, grads.shape[1])
 
 
 def no_col_path(block):
@@ -179,13 +184,14 @@
     row_pack = from_behind(row_part, "section", -1)
     section = lax.axis_index("section")
     place_z = section // 2
-    branch = jnp.where(section == lax.axis_size("section") - 1, 0, jnp.where(place_z == 5, 2, 1))
+    behaviour = jnp.where(place_z == 5, 2, 1)
+    branch = jnp.where(section == lax.axis_size("section") - 1, 0, behaviour)
     col_part = lax.switch(
         branch,
         [
             no_col_path,
-            functools.partial(col_path, (4,)),
-            functools.partial(col_path, (1, 3)),
+            functools.partial(col_path, 0),
+            functools.partial(col_path, 512),
         ],
         col_in,
     )

time: 126 us -> 135 us (1.071)
  the two profiles are of different devices: /device:TPU:449 before, /device:TPU:64 now
where the time goes in v6:
time: 135 us
  blocking collectives  115 us (85%)
  Pallas kernels  9.09 us (7%)
  waiting for transfers between devices  5.18 us (4%)
  starting transfers between devices  4.04 us (3%)
    all_to_all x2, blocking collectives, exchanged(): return lax.all_to_all(value, 'seq', split_axis=0, concat_axis=0, tiled=True)  115 us
    ppermute x2, waiting for transfers between devices, from_behind(): lax.ppermute(value, axis, [(source, source + steps) for source in range(l...  5.18 us
    pallas_call x1, Pallas kernels, row_grads(): pl.pallas_call(row_kernel, in_specs=[LEFT] * 4, out_specs=VMEM, out_shape...  4.96 us
    ppermute x2, starting transfers between devices, from_behind(): lax.ppermute(value, axis, [(source, source + steps) for source in range(l...  4.04 us
    pallas_call x1, Pallas kernels, col_grads(): pl.pallas_call(functools.partial(col_kernel, group), in_specs=[VMEM] * le...  2.87 us
  transfers between devices with their start and end apart: 2, of which 1 were waited for; matrix products, arithmetic and copies ran while one was open for 0% of the time, Pallas kernels for 6%

profile of v6, /device:TPU:64, one launch (start us, length us, event | category | flops | bytes accessed | tf_op | source)
XLA Modules:
  0.0 134.7 jit_solution(18174862809840195567)
XLA Ops:
  0.0 1.3 pad_maximum_fusion
  1.3 1.9 %collective-permute-start.1 = (bf16[256,2048]{1,0:T(8,128)(2,1)S(1)}, bf16[256,2048]{1,0:T(8,128)(2,1)S(1)}, u32[]{:S(2)}, u32[]{:S(2)}) collective-permute-start(bf16[256,2048]{1,0:T(8,128)(2,1)S(1)} %pad_maximum_fusion), channel_id=1, source_target_pairs={{32,0},{64,32},{96,64},{128,96},{160,128},{192,160},{224,192},{256... | collective-permute-start | bytes 3145736 | tf_op jit(solution)/shard_map/ppermute | solution.py:23
  3.2 5.0 %shard_map.82 = bf16[256,1536]{1,0:T(8,128)(2,1)} custom-call(bf16[256,512]{1,0:T(8,128)(2,1)} %bitcast.29, bf16[256,512]{1,0:T(8,128)(2,1)} %bitcast.30, bf16[256,512]{1,0:T(8,128)(2,1)} %bitcast.31, bf16[256,512]{1,0:T(8,128)(2,1)} %bitcast.32), custom_call_target="tpu_custom_call" | custom-call | flops 335544320 | bytes 1835008 | tf_op jit(solution)/shard_map/pallas_call | solution.py:93
  8.2 2.1 %collective-permute-start = (bf16[256,1536]{1,0:T(8,128)(2,1)}, bf16[256,1536]{1,0:T(8,128)(2,1)S(1)}, u32[]{:S(2)}, u32[]{:S(2)}) collective-permute-start(bf16[256,1536]{1,0:T(8,128)(2,1)} %shard_map.82), channel_id=1, source_target_pairs={{32,0},{64,32},{96,64},{128,96},{160,128},{192,160},{224,192},{256... | collective-permute-start | bytes 2359304 | tf_op jit(solution)/shard_map/ppermute | solution.py:23
  10.4 5.2 %collective-permute-done.1 = bf16[256,2048]{1,0:T(8,128)(2,1)S(1)} collective-permute-done((bf16[256,2048]{1,0:T(8,128)(2,1)S(1)}, bf16[256,2048]{1,0:T(8,128)(2,1)S(1)}, u32[]{:S(2)}, u32[]{:S(2)}) %collective-permute-start.1) | collective-permute-done | bytes 1048608 | tf_op jit(solution)/shard_map/ppermute | solution.py:23
  15.5 117.9 %conditional.1 = (bf16[256,1536]{1,0:T(8,128)(2,1)S(1)}) conditional(s32[]{:T(128)} %clamp.3, () %tuple.14, bf16[256,2048]{1,0:T(8,128)(2,1)S(1)} %collective-permute-done.1, bf16[256,2048]{1,0:T(8,128)(2,1)S(1)} %collective-permute-done.1), branch_computations={%region_0.1_spmd, %region_1.2_spmd, %region_2.3_spmd} | conditional | flops 335544320 | bytes 7864360 | solution.py:189
  15.5 53.4 %all_to_all.20 = bf16[32,8,2048]{2,1,0:T(8,128)(2,1)S(1)} all-to-all(bf16[32,8,2048]{2,1,0:T(8,128)(2,1)S(1)} %bitcast.26), channel_id=1, replica_groups=mesh['section'=16,'seq'=32] {'seq'}, dimensions={0} | all-to-all | bytes 2097152 | tf_op jit(solution)/shard_map/cond/branch_1_fun/all_to_all | solution.py:156
  68.9 2.9 %branch_1_fun.1 = bf16[256,1536]{1,0:T(8,128)(2,1)S(1)} custom-call(bf16[256,2048]{1,0:T(8,128)(2,1)S(1)} %bitcast.21), custom_call_target="tpu_custom_call" | custom-call | flops 335544320 | bytes 1835008 | tf_op jit(solution)/shard_map/cond/branch_1_fun/pallas_call | solution.py:125
  71.8 61.6 %all_to_all.21 = bf16[32,8,1536]{2,1,0:T(8,128)(2,1)S(1)} all-to-all(bf16[32,8,1536]{2,1,0:T(8,128)(2,1)S(1)} %bitcast.24), channel_id=1, replica_groups=mesh['section'=16,'seq'=32] {'seq'}, dimensions={0} | all-to-all | bytes 1572864 | tf_op jit(solution)/shard_map/cond/branch_1_fun/all_to_all | solution.py:156
  133.4 0.0 collective-permute-done.row_ref
  133.4 1.3 shard_map.83
Async XLA Ops:
  1.3 14.2 %collective-permute-start.1 = (bf16[256,2048]{1,0:T(8,128)(2,1)S(1)}, bf16[256,2048]{1,0:T(8,128)(2,1)S(1)}, u32[]{:S(2)}, u32[]{:S(2)}) collective-permute-start(bf16[256,2048]{1,0:T(8,128)(2,1)S(1)} %pad_maximum_fusion), channel_id=1, source_target_pairs={{32,0},{64,32},{96,64},{128,96},{160,128},{192,160},{224,192},{256... | collective-permute-start | bytes 3145736 | tf_op jit(solution)/shard_map/ppermute | solution.py:23
  8.2 125.2 %collective-permute-start = (bf16[256,1536]{1,0:T(8,128)(2,1)}, bf16[256,1536]{1,0:T(8,128)(2,1)S(1)}, u32[]{:S(2)}, u32[]{:S(2)}) collective-permute-start(bf16[256,1536]{1,0:T(8,128)(2,1)} %shard_map.82), channel_id=1, source_target_pairs={{32,0},{64,32},{96,64},{128,96},{160,128},{192,160},{224,192},{256... | collective-permute-start | bytes 2359304 | tf_op jit(solution)/shard_map/ppermute | solution.py:23
